TPU v7x, 512 devices: a whole 4x4x16 slice. The times are simulated.
512 devices in a mesh: dom: 128 (over z, y, core), rep: 4 (over x).
Axes of the slice: x: 4, y: 4, z: 16, core: 2. Of those that a mesh axis runs over, the one named last changes fastest.
Arguments:
- profiles: bfloat16 [300, 131072], P(None, 'dom'), may hold values from -6 to 6
- pack_index: int32 [128, 4, 128, 16], P('dom', 'rep'), may hold values from 0 to 1023, as said below
- obs_slot: int32 [4, 262144], P(None, ('dom', 'rep')), may hold values from 0 to 2047, as said below
- interp_weight: float32 [4, 262144], P(None, ('dom', 'rep')), may hold values from 0 to 1, as said below
- departures: float32 [100, 262144], P(None, ('dom', 'rep')), may hold values from -6 to 6
- w_in: bfloat16 [300, 512], replicated, may hold values from -0.375 to 0.375
- b_in: float32 [512], replicated, may hold values from -4 to 4
- w_mid: bfloat16 [512, 512], replicated, may hold values from -0.25 to 0.25
- b_mid: float32 [512], replicated, may hold values from -4 to 4
- w_out: bfloat16 [512, 100], replicated, may hold values from -0.25 to 0.25
Outputs:
- column_adjoint: float32 [300, 131072], P(None, ('dom', 'rep'))
Inputs may be any that keep to these rules, and one draw needn't show every extreme that they name: Local column numbers within the partition that holds pack_index's first index; the 16 columns of pack_index[o, r, d, :] are distinct and lie in quarter d % 4 of the partition, that is from (d % 4) * 256 to one less than (d % 4 + 1) * 256. `obs_slot`: slot o * 16 + j names the j-th column that the observation's segment and replica index take from partition o; where o lies more than 2 partitions from the segment's own index, counted cyclically, j < 4. `interp_weight`: bilinear weights: the four of an observation sum to one.
All inputs are finite; a program needn't handle non-finite values.
Results may differ from a plain program's by a relative error of at most 0.0057.
Values may be sent and summed in bfloat16 or wider, within the bound.
No kernel may reach another device: no remote copies, remote signals or barrier semaphores. Data moves between devices by JAX's collectives and lax.ppermute only.
A program may use at most 64 MiB of HBM per device.

v0:
```python
import jax
import jax.numpy as jnp
from jax import lax
from jax.sharding import PartitionSpec as P


def contract_first(matrix, values):
    return lax.dot_general(
        matrix, values, (((0,), (0,)), ((), ())), preferred_element_type=jnp.float32
    )


def interpolate(fetched, obs_slot, interp_weight):
    summed = jnp.zeros((fetched.shape[0], obs_slot.shape[1]), jnp.float32)
    for corner in range(4):
        summed = summed + interp_weight[corner] * jnp.take(
            fetched, obs_slot[corner], axis=1
        ).astype(jnp.float32)
    return summed.astype(jnp.bfloat16)


def network_adjoint(inputs, departures, w_in, b_in, w_mid, b_mid, w_out):
    z_one = contract_first(w_in, inputs) + b_in[:, None]
    act_one = jnp.tanh(z_one).astype(jnp.bfloat16)
    z_two = contract_first(w_mid, act_one) + b_mid[:, None]
    cot_out = departures.astype(jnp.bfloat16)
    g_two = (
        jnp.dot(w_out, cot_out, preferred_element_type=jnp.float32) * (1.0 - jnp.tanh(z_two) ** 2)
    ).astype(jnp.bfloat16)
    g_one = (
        jnp.dot(w_mid, g_two, preferred_element_type=jnp.float32) * (1.0 - jnp.tanh(z_one) ** 2)
    ).astype(jnp.bfloat16)
    return jnp.dot(w_in, g_one, preferred_element_type=jnp.float32)


def spread_slots(g_inputs, obs_slot, interp_weight, slot_total):
    slot_adjoint = jnp.zeros((g_inputs.shape[0], slot_total), jnp.float32)
    for corner in range(4):
        slot_adjoint = slot_adjoint.at[:, obs_slot[corner]].add(interp_weight[corner] * g_inputs)
    return slot_adjoint


def body(
    profiles, pack_index, obs_slot, interp_weight, departures, w_in, b_in, w_mid, b_mid, w_out
):
    send_lists = pack_index[0, 0]
    packed = jnp.take(profiles, send_lists.reshape(-1), axis=1)
    fetched = lax.all_to_all(packed, "dom", split_axis=1, concat_axis=1, tiled=True)
    inputs = interpolate(fetched, obs_slot, interp_weight)
    g_inputs = network_adjoint(inputs, departures, w_in, b_in, w_mid, b_mid, w_out)
    slot_adjoint = spread_slots(g_inputs, obs_slot, interp_weight, fetched.shape[1])
    main_values = lax.all_to_all(slot_adjoint, "dom", split_axis=1, concat_axis=1, tiled=True)
    column_adjoint = jnp.zeros(profiles.shape, jnp.float32)
    column_adjoint = column_adjoint.at[:, send_lists.reshape(-1)].add(main_values)
    return lax.psum_scatter(column_adjoint, "rep", scatter_dimension=1, tiled=True)


def solution(mesh):
    placed = (
        P(None, "dom"),
        P("dom", "rep", None, None),
        P(None, ("dom", "rep")),
        P(None, ("dom", "rep")),
        P(None, ("dom", "rep")),
        P(),
        P(),
        P(),
        P(),
        P(),
    )
    return jax.shard_map(
        body, mesh=mesh, in_specs=placed, out_specs=P(None, ("dom", "rep")), check_vma=False
    )
```

profile of v0, /device:TPU:1, one launch (start us, length us, event | category | flops | bytes accessed | tf_op | source)
XLA Modules:
  0.0 363.7 jit_solution(7984136721723804361)
XLA Ops:
  6.5 0.9 copy.18
  7.4 0.7 compare_and_fusion
  8.1 0.1 reshape_squeeze.6
  8.2 1.4 copy.20
  9.7 0.1 copy.19
  9.8 7.5 %gather_fusion = bf16[2048,300]{1,0:T(8,128)(2,1)S(1)} fusion(bf16[300,1024]{0,1:T(8,128)(2,1)S(1)} %copy.20, s32[2048]{0:T(1024)S(1)} %broadcast_clamp_fusion), kind=kCustom, calls=%fused_computation.4 | custom fusion | bytes 2465792 | tf_op jit(solution)/shard_map/jit(_take)/gather | solution.py:47
  17.2 0.0 copy-start.5
  17.3 1.4 broadcast_select_fusion
  18.7 20.6 %all-to-all-start = ((bf16[300,128,16]{0,2,1:T(8,128)(2,1)}), bf16[300,128,16]{0,2,1:T(8,128)(2,1)S(1)}, u32[]{:S(2)}, u32[]{:S(2)}) async-start(bf16[300,128,16]{0,2,1:T(8,128)(2,1)} %broadcast_select_fusion), calls=%async_computation | async-start | bytes 3145728 | tf_op jit(solution)/shard_map/all_to_all | solution.py:48
  39.3 0.0 reduce-scatter.2.cloned.1.call-start
  39.5 0.3 fusion.34
  39.9 72.4 %all-to-all-done = bf16[300,128,16]{0,2,1:T(8,128)(2,1)S(1)} async-done(((bf16[300,128,16]{0,2,1:T(8,128)(2,1)}), bf16[300,128,16]{0,2,1:T(8,128)(2,1)S(1)}, u32[]{:S(2)}, u32[]{:S(2)}) %all-to-all-start) | async-done | bytes 1228832 | tf_op jit(solution)/shard_map/all_to_all | solution.py:48
  112.2 2.6 gather_fusion.1
  114.8 2.6 gather_fusion.2
  117.4 2.6 gather_fusion.3
  119.9 2.6 gather_fusion.4
  122.5 2.5 fusion.7
  125.0 1.3 fusion.8
  126.4 3.0 broadcast_multiply_fusion
  129.3 1.1 copy.21
  130.5 1.3 copy.22
  131.8 0.3 copy.23
  132.1 0.3 copy.24
  132.4 6.0 %scatter_custom_fusion = f32[300,2048]{0,1:T(8,128)} fusion(s32[512]{0:T(512)S(1)} %bitcast.95, f32[512,300]{1,0:T(8,128)} %copy.21, f32[]{:T(128)} %constant.8.clone.1), kind=kCustom, calls=%fused_computation.10 | custom fusion | flops 153600 | bytes 2458112 | tf_op jit(solution)/shard_map/scatter-add | solution.py:39
  138.3 7.1 %scatter_fusion = f32[300,2048]{0,1:T(8,128)} fusion(f32[300,2048]{0,1:T(8,128)} %scatter_custom_fusion, s32[512]{0:T(512)S(1)} %bitcast.94, f32[512,300]{1,0:T(8,128)S(1)} %copy.22), kind=kCustom, calls=%fused_computation.6 | custom fusion | flops 153600 | bytes 1845248 | tf_op jit(solution)/shard_map/scatter-add | solution.py:39
  145.4 7.1 %scatter_fusion.1 = f32[300,2048]{0,1:T(8,128)} fusion(f32[300,2048]{0,1:T(8,128)} %scatter_fusion, s32[512]{0:T(512)S(1)} %bitcast.93, f32[512,300]{1,0:T(8,128)S(1)} %copy.23), kind=kCustom, calls=%fused_computation.7 | custom fusion | flops 153600 | bytes 1845248 | tf_op jit(solution)/shard_map/scatter-add | solution.py:39
  152.5 7.1 %scatter_fusion.2 = f32[300,2048]{0,1:T(8,128)} fusion(f32[300,2048]{0,1:T(8,128)} %scatter_fusion.1, s32[512]{0:T(512)S(1)} %bitcast.92, f32[512,300]{1,0:T(8,128)S(1)} %copy.24), kind=kCustom, calls=%fused_computation.8 | custom fusion | flops 153600 | bytes 1845248 | tf_op jit(solution)/shard_map/scatter-add | solution.py:39
  159.5 152.1 %all_to_all.21 = f32[300,128,16]{0,2,1:T(8,128)} all-to-all(f32[300,128,16]{0,2,1:T(8,128)} %bitcast.67), channel_id=1, replica_groups=mesh['dom'=128,'rep'=4] {'dom'}, dimensions={1} | all-to-all | bytes 4915200 | tf_op jit(solution)/shard_map/all_to_all | solution.py:52
  311.7 14.4 %scatter_custom_fusion.4 = f32[300,1024]{0,1:T(8,128)} fusion(s32[2048]{0:T(1024)S(1)} %bitcast.75, f32[2048,300]{1,0:T(8,128)} %bitcast.73, f32[]{:T(128)} %constant.8.clone.1), kind=kCustom, calls=%fused_computation.28 | custom fusion | flops 614400 | bytes 1229312 | tf_op jit(solution)/shard_map/scatter-add | solution.py:54
  326.0 0.0 reduce-scatter.2.cloned.1.call-update
  326.1 28.9 %reduce-scatter.2.cloned.1.call-done = f32[300,256]{0,1:T(8,128)} async-done(((f32[300,1024]{0,1:T(8,128)}), f32[300,256]{0,1:T(8,128)}) %reduce-scatter.2.cloned.1.call-update) | async-done | bytes 307216 | tf_op jit(solution)/shard_map/reduce_scatter | solution.py:55
  355.0 1.9 copy.25
  (32 shorter events, 0.1 us)
Async XLA Ops:
  6.5 118.5 %copy-start = (bf16[512,512]{1,0:T(8,128)(2,1)S(1)}, bf16[512,512]{1,0:T(8,128)(2,1)}, u32[]{:S(2)}) copy-start(bf16[512,512]{1,0:T(8,128)(2,1)} %param.19) | copy-start | bytes 1572868
  17.2 22.1 %copy-start.5 = (s32[4,512]{1,0:T(4,128)S(1)}, s32[4,512]{1,0:T(4,128)}, u32[]{:S(2)}) copy-start(s32[4,512]{1,0:T(4,128)} %param.14) | copy-start | bytes 24580
  17.3 22.2 %copy-start.6 = (f32[4,512]{1,0:T(4,128)S(1)}, f32[4,512]{1,0:T(4,128)}, u32[]{:S(2)}) copy-start(f32[4,512]{1,0:T(4,128)} %param.15) | copy-start | bytes 24580
  17.3 22.3 %copy-start.3 = (f32[100,512]{1,0:T(8,128)S(1)}, f32[100,512]{1,0:T(8,128)}, u32[]{:S(2)}) copy-start(f32[100,512]{1,0:T(8,128)} %param.16) | copy-start | bytes 614404
  17.3 22.2 %copy-start.4 = (bf16[512,100]{0,1:T(8,128)(2,1)S(1)}, bf16[512,100]{0,1:T(8,128)(2,1)}, u32[]{:S(2)}) copy-start(bf16[512,100]{0,1:T(8,128)(2,1)} %param.21) | copy-start | bytes 307204
  18.7 93.5 %all-to-all-start = ((bf16[300,128,16]{0,2,1:T(8,128)(2,1)}), bf16[300,128,16]{0,2,1:T(8,128)(2,1)S(1)}, u32[]{:S(2)}, u32[]{:S(2)}) async-start(bf16[300,128,16]{0,2,1:T(8,128)(2,1)} %broadcast_select_fusion), calls=%async_computation | async-start | bytes 3145728 | tf_op jit(solution)/shard_map/all_to_all | solution.py:48
  39.3 315.7 %reduce-scatter.2.cloned.1.call-start = ((), (), s32[]{:S(2)}) async-start(), calls=%async_computation.3 | async-start | bytes 1966080 | tf_op jit(solution)/shard_map/reduce_scatter | solution.py:55
  117.4 5.1 %copy-start.2 = (bf16[300,512]{1,0:T(8,128)(2,1)S(1)}, bf16[300,512]{1,0:T(8,128)(2,1)}, u32[]{:S(2)}) copy-start(bf16[300,512]{1,0:T(8,128)(2,1)} %param.17) | copy-start | bytes 921604
  117.4 5.1 %copy-start.8 = (f32[512]{0:T(512)S(1)}, f32[512]{0:T(512)}, u32[]{:S(2)}) copy-start(f32[512]{0:T(512)} %param.18) | copy-start | bytes 6148
  122.5 2.5 copy-start.7
  129.3 2.5 copy-start.1
Sparse Core Ops, SparseCore 0:
  326.2 28.7 reduce-scatter.1
where the time goes:
time: 364 us
  blocking collectives  152 us (42%)
  waiting for transfers between devices  101 us (28%)
  other arithmetic  43.7 us (12%)
  local copies, waits for them, and re-layouts  25.2 us (7%)
  starting transfers between devices  20.6 us (6%)
  between operations  13.7 us (4%)
  matrix products  7.11 us (2%)
    all_to_all x1, blocking collectives, body(): lax.all_to_all(slot_adjoint, 'dom', split_axis=1, concat_axis=1, tiled=True)  152 us
    all_to_all x1, waiting for transfers between devices, body(): lax.all_to_all(packed, 'dom', split_axis=1, concat_axis=1, tiled=True)  72.4 us
    reduce_scatter x1, waiting for transfers between devices, body(): lax.psum_scatter(column_adjoint, 'rep', scatter_dimension=1, tiled=True)  28.9 us
    scatter-add x4, other arithmetic, spread_slots(): slot_adjoint.at[:, obs_slot[corner]].add(interp_weight[corner] * g_inputs)  27.2 us
    all_to_all x1, starting transfers between devices, body(): lax.all_to_all(packed, 'dom', split_axis=1, concat_axis=1, tiled=True)  20.6 us
    scatter-add x1, other arithmetic, body(): column_adjoint.at[:, send_lists.reshape(-1)].add(main_values)  14.4 us
    gather x4, local copies, waits for them, and re-layouts, interpolate(): jnp.take(fetched, obs_slot[corner], axis=1).astype(jnp.float32)  10.3 us
    gather x1, local copies, waits for them, and re-layouts, body(): packed = jnp.take(profiles, send_lists.reshape(-1), axis=1)  7.46 us
  transfers between devices with their start and end apart: 2, of which 2 were waited for; matrix products, arithmetic and copies ran while one was open for 0% of the time, Pallas kernels for 0%

commit v1 on v0

v1 whole, which is shorter than its diff:
```python
import jax
import jax.numpy as jnp
from jax import lax
from jax.experimental import pallas as pl
from jax.experimental.pallas import tpu as pltpu
from jax.sharding import PartitionSpec as P

F32 = jnp.float32
BF16 = jnp.bfloat16
N_DOM = 128
N_REP = 4
CAP = 16
FAR = 4
REACH = 2
FEAT = 300
WIDE = FEAT + 1
PAIR = 2 * WIDE
FAR_ROWS = N_DOM * FAR // 2
NEAR_ROWS = (CAP - FAR) // 2
NEAR_ALL = (2 * REACH + 1) * NEAR_ROWS
ROWS = 288
QUARTER = 256
COLS = 1024


def dot(a, b, ca, cb):
    return lax.dot_general(a, b, (((ca,), (cb,)), ((), ())), preferred_element_type=F32)


def pack_kernel(idx_ref, prof_ref, far_ref, near_ref):
    prof = prof_ref[...]
    lane = lax.broadcasted_iota(jnp.int32, (ROWS, COLS), 1)
    place = (lax.broadcasted_iota(jnp.int32, (8, COLS), 1) % QUARTER).astype(F32).astype(BF16)
    halves = []
    for p in range(2):
        pick = jnp.where(idx_ref[:, p : p + 1] == lane, 1.0, 0.0).astype(BF16)
        halves.append(dot(pick, prof, 1, 1))
        halves.append(dot(pick, place, 1, 1)[:, :1])
    rows = jnp.concatenate(halves, axis=1).astype(BF16)
    far_ref[...] = rows[:FAR_ROWS]
    near_ref[...] = rows[FAR_ROWS:]


def prep_kernel(
    dom_ref, slot_ref, weight_ref, dep_ref, w_in_ref, w_mid_ref, w_out_ref,
    hi_ref, lo_ref, hi_t_ref, lo_t_ref, seed_ref, w_in_t_ref, w_mid_t_ref,
):
    slot = slot_ref[...]
    owner = slot // CAP
    j = slot % CAP
    apart = (owner - dom_ref[0] + REACH) % N_DOM
    row = jnp.where(
        j < FAR, owner * (FAR // 2) + j // 2, FAR_ROWS + apart * NEAR_ROWS + (j - FAR) // 2
    )
    obs = slot.shape[1]
    index = lax.broadcasted_iota(jnp.int32, (ROWS, obs), 0)
    for p in range(2):
        mine = jnp.where(j % 2 == p, row, -1)
        acc = jnp.zeros((ROWS, obs), F32)
        for k in range(4):
            acc = acc + jnp.where(mine[k : k + 1] == index, weight_ref[k : k + 1], 0.0)
        hi = acc.astype(BF16)
        lo = acc - hi.astype(F32)
        hi_ref[p] = hi
        lo_ref[p] = lo.astype(BF16)
        hi_t_ref[p] = acc.T.astype(BF16)
        lo_t_ref[p] = lo.T.astype(BF16)
    seed_ref[...] = dot(dep_ref[...].astype(BF16), w_out_ref[...], 0, 1)
    w_in_t_ref[...] = w_in_ref[...].T
    w_mid_t_ref[...] = w_mid_ref[...].T


def main_kernel(
    far_ref, near_ref, hi_ref, lo_ref, hi_t_ref, lo_t_ref, seed_ref,
    w_in_ref, b_in_ref, w_mid_ref, b_mid_ref, w_in_t_ref, w_mid_t_ref,
    far_out_ref, near_out_ref,
):
    fetched = jnp.concatenate([far_ref[...], near_ref[...]], axis=0)
    summed = None
    for p in range(2):
        values = fetched[:, p * WIDE : p * WIDE + FEAT]
        part = dot(hi_t_ref[p], values, 1, 0) + dot(lo_t_ref[p], values, 1, 0)
        summed = part if summed is None else summed + part
    inputs = summed.astype(BF16)
    t_one = jnp.tanh(dot(inputs, w_in_ref[...], 1, 0) + b_in_ref[...])
    t_two = jnp.tanh(dot(t_one.astype(BF16), w_mid_ref[...], 1, 0) + b_mid_ref[...])
    g_two = (seed_ref[...] * (1.0 - t_two * t_two)).astype(BF16)
    g_one = (dot(g_two, w_mid_t_ref[...], 1, 0) * (1.0 - t_one * t_one)).astype(BF16)
    g_inputs = dot(g_one, w_in_t_ref[...], 1, 0)
    g_hi = g_inputs.astype(BF16)
    g_lo = (g_inputs - g_hi.astype(F32)).astype(BF16)
    halves = []
    for p in range(2):
        halves.append(dot(hi_ref[p], g_hi, 1, 0) + dot(lo_ref[p], g_hi, 1, 0) + dot(hi_ref[p], g_lo, 1, 0))
        halves.append(fetched[:, p * WIDE + FEAT : (p + 1) * WIDE].astype(F32))
    rows = jnp.concatenate(halves, axis=1).astype(BF16)
    far_out_ref[...] = rows[:FAR_ROWS]
    near_out_ref[...] = rows[FAR_ROWS:]


def final_kernel(got_ref, out_ref):
    got = got_ref[...]
    lane = lax.broadcasted_iota(jnp.int32, (got.shape[0], QUARTER), 1).astype(F32)
    total = None
    for p in range(2):
        place = got[:, p * WIDE + FEAT : (p + 1) * WIDE].astype(F32)
        pick = jnp.where(place == lane, 1.0, 0.0).astype(BF16)
        part = dot(got[:, p * WIDE : p * WIDE + FEAT], pick, 0, 0)
        total = part if total is None else total + part
    out_ref[...] = total


def shape(dims, dtype):
    return jax.ShapeDtypeStruct(dims, dtype)


def exchange_near(near, sign):
    moved = []
    for i in range(2 * REACH + 1):
        step = sign * (i - REACH)
        block = near[i]
        if step:
            block = lax.ppermute(block, "dom", [(a, (a + step) % N_DOM) for a in range(N_DOM)])
        moved.append(block)
    return moved


def body(
    profiles, pack_index, obs_slot, interp_weight, departures, w_in, b_in, w_mid, b_mid, w_out
):
    dom = lax.axis_index("dom")
    lists = pack_index[0, 0]
    around = jnp.concatenate([lists[-REACH:], lists, lists[:REACH]], axis=0)
    near_lists = lax.dynamic_slice_in_dim(around, dom, 2 * REACH + 1, 0)
    idx = jnp.concatenate(
        [
            lists[:, :FAR].reshape(FAR_ROWS, 2),
            near_lists[:, FAR:].reshape(NEAR_ALL, 2),
            jnp.zeros((ROWS - FAR_ROWS - NEAR_ALL, 2), jnp.int32),
        ],
        axis=0,
    )
    extra = ROWS - FAR_ROWS
    far, near = pl.pallas_call(
        pack_kernel,
        out_shape=(shape((FAR_ROWS, PAIR), BF16), shape((extra, PAIR), BF16)),
        name="pack",
    )(idx, profiles)

    obs = obs_slot.shape[1]
    hidden = w_mid.shape[0]
    smem = pl.BlockSpec(memory_space=pltpu.SMEM)
    vmem = pl.BlockSpec(memory_space=pltpu.VMEM)
    hi, lo, hi_t, lo_t, seed, w_in_t, w_mid_t = pl.pallas_call(
        prep_kernel,
        out_shape=(
            shape((2, ROWS, obs), BF16), shape((2, ROWS, obs), BF16),
            shape((2, obs, ROWS), BF16), shape((2, obs, ROWS), BF16),
            shape((obs, hidden), F32), shape((hidden, FEAT), BF16), shape((hidden, hidden), BF16),
        ),
        in_specs=[smem] + [vmem] * 6,
        name="prep",
    )(dom.reshape(1).astype(jnp.int32), obs_slot, interp_weight, departures, w_in, w_mid, w_out)

    near_parts = near[:NEAR_ALL].reshape(2 * REACH + 1, NEAR_ROWS // 2, 2, PAIR)
    got_near = exchange_near(near_parts, 1)
    got_far = lax.all_to_all(far.reshape(N_DOM, FAR // 2, PAIR), "dom", 0, 0, tiled=True)
    near_rows = jnp.concatenate(got_near[::-1], axis=0).reshape(NEAR_ALL, PAIR)
    near_rows = jnp.pad(near_rows, ((0, extra - NEAR_ALL), (0, 0)))

    far_adj, near_adj = pl.pallas_call(
        main_kernel,
        out_shape=(shape((FAR_ROWS, PAIR), BF16), shape((extra, PAIR), BF16)),
        name="main",
    )(
        got_far.reshape(FAR_ROWS, PAIR), near_rows, hi, lo, hi_t, lo_t, seed,
        w_in, b_in.reshape(1, -1), w_mid, b_mid.reshape(1, -1), w_in_t, w_mid_t,
    )

    near_parts = near_adj[:NEAR_ALL].reshape(2 * REACH + 1, NEAR_ROWS // 2, 2, PAIR)
    back_near = exchange_near(near_parts, 1)[::-1]
    back_far = lax.all_to_all(far_adj.reshape(N_DOM, FAR // 2, PAIR), "dom", 0, 0, tiled=True)
    stacked = jnp.stack(back_near[:N_REP] * 2)
    first = lax.dynamic_slice_in_dim(stacked, (REACH - dom) % N_REP, N_REP, 0)
    owner = (jnp.arange(N_REP) == (dom + REACH) % N_REP).reshape(N_REP, 1, 1, 1)
    second = jnp.where(owner, back_near[N_REP][None], jnp.zeros((), BF16))
    by_quarter = back_far.reshape(N_DOM // N_REP, N_REP, FAR // 2, PAIR).transpose(1, 0, 2, 3)
    outgoing = jnp.concatenate([by_quarter, first, second], axis=1)
    got = lax.all_to_all(outgoing, "rep", 0, 0, tiled=True)
    return pl.pallas_call(
        final_kernel, out_shape=shape((FEAT, QUARTER), F32), name="final"
    )(got.reshape(-1, PAIR))


def solution(mesh):
    placed = (
        P(None, "dom"),
        P("dom", "rep", None, None),
        P(None, ("dom", "rep")),
        P(None, ("dom", "rep")),
        P(None, ("dom", "rep")),
        P(),
        P(),
        P(),
        P(),
        P(),
    )
    return jax.shard_map(
        body, mesh=mesh, in_specs=placed, out_specs=P(None, ("dom", "rep")), check_vma=False
    )
```

time: 364 us -> 126 us (0.35)
  the two profiles are of different devices: /device:TPU:1 before, /device:TPU:32 now
where the time goes in v1:
time: 126 us
  starting transfers between devices  59 us (47%)
  waiting for transfers between devices  25.7 us (20%)
  Pallas kernels  16.3 us (13%)
  blocking collectives  12.7 us (10%)
  local copies, waits for them, and re-layouts  9.94 us (8%)
  other arithmetic  1.53 us (1%)
    ppermute x8, starting transfers between devices, exchange_near(): lax.ppermute(block, 'dom', [(a, (a + step) % N_DOM) for a in range(N_DOM)])  28.3 us
    all_to_all x1, starting transfers between devices, body(): lax.all_to_all(far.reshape(N_DOM, FAR // 2, PAIR), 'dom', 0, 0, tiled=True)  19.3 us
    all_to_all x1, blocking collectives, body(): got = lax.all_to_all(outgoing, 'rep', 0, 0, tiled=True)  12.7 us
    all_to_all x1, waiting for transfers between devices, body(): lax.all_to_all(far_adj.reshape(N_DOM, FAR // 2, PAIR), 'dom', 0, 0, tiled...  12.4 us
    all_to_all x1, starting transfers between devices, body(): lax.all_to_all(far_adj.reshape(N_DOM, FAR // 2, PAIR), 'dom', 0, 0, tiled...  11.4 us
    ppermute x8, waiting for transfers between devices, exchange_near(): lax.ppermute(block, 'dom', [(a, (a + step) % N_DOM) for a in range(N_DOM)])  7.7 us
    pallas_call x1, Pallas kernels, body(): pl.pallas_call(main_kernel, out_shape=(shape((FAR_ROWS, PAIR), BF16), sha...  6.69 us
    all_to_all x1, waiting for transfers between devices, body(): lax.all_to_all(far.reshape(N_DOM, FAR // 2, PAIR), 'dom', 0, 0, tiled=True)  5.53 us
  transfers between devices with their start and end apart: 10, of which 3 were waited for; matrix products, arithmetic and copies ran while one was open for 3% of the time, Pallas kernels for 3%

profile of v1, /device:TPU:32, one launch (start us, length us, event | category | flops | bytes accessed | tf_op | source)
XLA Modules:
  0.0 125.5 jit_solution(4239293307915708295)
XLA Ops:
  0.0 0.7 copy-done.1
  0.9 0.1 copy.46
  1.0 0.1 copy.41
  1.3 0.8 add_add_fusion.idx_ref
  2.1 3.1 %pack.1 = (bf16[256,602]{1,0:T(8,128)(2,1)}, bf16[32,602]{1,0:T(8,128)(2,1)}) custom-call(s32[288,2]{1,0:T(8,128)} %add_add_fusion.idx_ref, bf16[300,1024]{1,0:T(8,128)(2,1)} %prof_ref.1), custom_call_target="tpu_custom_call" | custom-call | tf_op jit(solution)/shard_map/pack/pallas_call | solution.py:144
  5.2 1.8 %reshape.64 = bf16[128,2,602]{2,1,0:T(2,128)(2,1)} reshape(bf16[256,602]{1,0:T(8,128)(2,1)} %get-tuple-element.16) | data formatting | bytes 616448 | tf_op jit(solution)/shard_map/reshape | solution.py:167
  7.1 19.3 %all-to-all-start = ((bf16[128,2,602]{2,1,0:T(2,128)(2,1)}), bf16[128,2,602]{2,1,0:T(2,128)(2,1)S(1)}, u32[]{:S(2)}, u32[]{:S(2)}) async-start(bf16[128,2,602]{2,1,0:T(2,128)(2,1)} %reshape.64), calls=%async_computation | async-start | bytes 655360 | tf_op jit(solution)/shard_map/all_to_all | solution.py:167
  26.4 3.4 %collective-permute-start = (bf16[3,2,602]{2,1,0:T(2,128)(2,1)S(1)}, bf16[3,2,602]{2,1,0:T(2,128)(2,1)S(1)}, u32[]{:S(2)}, u32[]{:S(2)}) collective-permute-start(bf16[3,2,602]{2,1,0:T(2,128)(2,1)S(1)} %squeeze.31), channel_id=1, source_target_pairs={{0,8},{4,12},{8,16},{12,20},{16,24},{20,28},{24,32},{28,36},{32,40... | collective-permute-start | bytes 21680 | tf_op jit(solution)/shard_map/ppermute | solution.py:123
  29.8 1.9 %collective-permute-start.1 = (bf16[3,2,602]{2,1,0:T(2,128)(2,1)S(1)}, bf16[3,2,602]{2,1,0:T(2,128)(2,1)S(1)}, u32[]{:S(2)}, u32[]{:S(2)}) collective-permute-start(bf16[3,2,602]{2,1,0:T(2,128)(2,1)S(1)} %squeeze.32), channel_id=1, source_target_pairs={{0,4},{4,8},{8,12},{12,16},{16,20},{20,24},{24,28},{28,32},{32,36}... | collective-permute-start | bytes 21680 | tf_op jit(solution)/shard_map/ppermute | solution.py:123
  31.8 5.8 %collective-permute-start.2 = (bf16[3,2,602]{2,1,0:T(2,128)(2,1)S(1)}, bf16[3,2,602]{2,1,0:T(2,128)(2,1)S(1)}, u32[]{:S(2)}, u32[]{:S(2)}) collective-permute-start(bf16[3,2,602]{2,1,0:T(2,128)(2,1)S(1)} %squeeze.34), channel_id=1, source_target_pairs={{0,508},{4,0},{8,4},{12,8},{16,12},{20,16},{24,20},{28,24},{32,28}... | collective-permute-start | bytes 21680 | tf_op jit(solution)/shard_map/ppermute | solution.py:123
  37.6 2.5 %collective-permute-start.3 = (bf16[3,2,602]{2,1,0:T(2,128)(2,1)S(1)}, bf16[3,2,602]{2,1,0:T(2,128)(2,1)S(1)}, u32[]{:S(2)}, u32[]{:S(2)}) collective-permute-start(bf16[3,2,602]{2,1,0:T(2,128)(2,1)S(1)} %squeeze.35), channel_id=1, source_target_pairs={{0,504},{4,508},{8,0},{12,4},{16,8},{20,12},{24,16},{28,20},{32,24... | collective-permute-start | bytes 21680 | tf_op jit(solution)/shard_map/ppermute | solution.py:123
  40.1 0.8 copy.47.w_out_ref
  40.8 4.2 %prep.1 = (bf16[2,288,512]{2,1,0:T(8,128)(2,1)}, bf16[2,288,512]{2,1,0:T(8,128)(2,1)}, bf16[2,512,288]{2,1,0:T(8,128)(2,1)}, bf16[2,512,288]{2,1,0:T(8,128)(2,1)...) custom-call(s32[1]{0:T(128)} %bitcast.3.dom_ref, s32[4,512]{1,0:T(4,128)} %slot_ref.1, ...), custom_call_target="tpu_custom_call" | custom-call | tf_op jit(solution)/shard_map/prep/pallas_call | solution.py:154
  45.2 0.6 pad.4.near_ref
  45.9 5.5 %all-to-all-done = bf16[128,2,602]{2,1,0:T(2,128)(2,1)S(1)} async-done(((bf16[128,2,602]{2,1,0:T(2,128)(2,1)}), bf16[128,2,602]{2,1,0:T(2,128)(2,1)S(1)}, u32[]{:S(2)}, u32[]{:S(2)}) %all-to-all-start) | async-done | bytes 308256 | tf_op jit(solution)/shard_map/all_to_all | solution.py:167
  51.4 1.0 reshape.65.far_ref
  52.4 6.7 %main.1 = (bf16[256,602]{1,0:T(8,128)(2,1)}, bf16[32,602]{1,0:T(8,128)(2,1)}) custom-call(bf16[256,602]{1,0:T(8,128)(2,1)} %reshape.65.far_ref, bf16[32,602]{1,0:T(8,128)(2,1)} %pad.4.near_ref, bf16[2,288,512]{2,1,0:T(8,128)(2,1)} %get-tuple-element.18.hi_ref, bf16[2,288,512]{2,1,0:T(8,128)(2,1)} %get-tuple-element.19.lo_ref, ...), custom_call_target="tpu_custom_call" | custom-call | tf_op jit(solution)/shard_map/main/pallas_call | solution.py:171
  59.1 0.8 fusion.2
  59.9 2.5 %collective-permute-start.4 = (bf16[3,2,602]{2,1,0:T(2,128)(2,1)S(1)}, bf16[3,2,602]{2,1,0:T(2,128)(2,1)S(1)}, u32[]{:S(2)}, u32[]{:S(2)}) collective-permute-start(bf16[3,2,602]{2,1,0:T(2,128)(2,1)S(1)} %squeeze.36), channel_id=1, source_target_pairs={{0,8},{4,12},{8,16},{12,20},{16,24},{20,28},{24,32},{28,36},{32,40... | collective-permute-start | bytes 21680 | tf_op jit(solution)/shard_map/ppermute | solution.py:123
  62.5 1.9 %collective-permute-start.5 = (bf16[3,2,602]{2,1,0:T(2,128)(2,1)S(1)}, bf16[3,2,602]{2,1,0:T(2,128)(2,1)S(1)}, u32[]{:S(2)}, u32[]{:S(2)}) collective-permute-start(bf16[3,2,602]{2,1,0:T(2,128)(2,1)S(1)} %squeeze.37), channel_id=1, source_target_pairs={{0,4},{4,8},{8,12},{12,16},{16,20},{20,24},{24,28},{28,32},{32,36}... | collective-permute-start | bytes 21680 | tf_op jit(solution)/shard_map/ppermute | solution.py:123
  64.5 5.8 %collective-permute-start.6 = (bf16[3,2,602]{2,1,0:T(2,128)(2,1)S(1)}, bf16[3,2,602]{2,1,0:T(2,128)(2,1)S(1)}, u32[]{:S(2)}, u32[]{:S(2)}) collective-permute-start(bf16[3,2,602]{2,1,0:T(2,128)(2,1)S(1)} %squeeze.38), channel_id=1, source_target_pairs={{0,508},{4,0},{8,4},{12,8},{16,12},{20,16},{24,20},{28,24},{32,28}... | collective-permute-start | bytes 21680 | tf_op jit(solution)/shard_map/ppermute | solution.py:123
  70.3 1.8 %reshape.70 = bf16[128,2,602]{2,1,0:T(2,128)(2,1)} reshape(bf16[256,602]{1,0:T(8,128)(2,1)} %get-tuple-element.25) | data formatting | bytes 616448 | tf_op jit(solution)/shard_map/reshape | solution.py:182
  72.1 11.4 %all-to-all-start.1 = ((bf16[128,2,602]{2,1,0:T(2,128)(2,1)}), bf16[128,2,602]{2,1,0:T(2,128)(2,1)S(1)}, u32[]{:S(2)}, u32[]{:S(2)}) async-start(bf16[128,2,602]{2,1,0:T(2,128)(2,1)} %reshape.70), calls=%async_computation.1 | async-start | bytes 655360 | tf_op jit(solution)/shard_map/all_to_all | solution.py:182
  83.6 4.6 %collective-permute-start.7 = (bf16[3,2,602]{2,1,0:T(2,128)(2,1)S(1)}, bf16[3,2,602]{2,1,0:T(2,128)(2,1)S(1)}, u32[]{:S(2)}, u32[]{:S(2)}) collective-permute-start(bf16[3,2,602]{2,1,0:T(2,128)(2,1)S(1)} %squeeze.39), channel_id=1, source_target_pairs={{0,504},{4,508},{8,0},{12,4},{16,8},{20,12},{24,16},{28,20},{32,24... | collective-permute-start | bytes 21680 | tf_op jit(solution)/shard_map/ppermute | solution.py:123
  88.4 7.7 %collective-permute-done.7 = bf16[3,2,602]{2,1,0:T(2,128)(2,1)S(1)} collective-permute-done((bf16[3,2,602]{2,1,0:T(2,128)(2,1)S(1)}, bf16[3,2,602]{2,1,0:T(2,128)(2,1)S(1)}, u32[]{:S(2)}, u32[]{:S(2)}) %collective-permute-start.7) | collective-permute-done | bytes 7256 | tf_op jit(solution)/shard_map/ppermute | solution.py:123
  96.1 0.1 broadcast_select_fusion
  96.2 12.4 %all-to-all-done.1 = bf16[128,2,602]{2,1,0:T(2,128)(2,1)S(1)} async-done(((bf16[128,2,602]{2,1,0:T(2,128)(2,1)}), bf16[128,2,602]{2,1,0:T(2,128)(2,1)S(1)}, u32[]{:S(2)}, u32[]{:S(2)}) %all-to-all-start.1) | async-done | bytes 308256 | tf_op jit(solution)/shard_map/all_to_all | solution.py:182
  108.6 0.6 pad_maximum_fusion
  109.2 0.3 copy.50
  109.5 12.7 %all_to_all.15 = bf16[4,38,2,602]{3,2,1,0:T(2,128)(2,1)S(1)} all-to-all(bf16[4,38,2,602]{3,2,1,0:T(2,128)(2,1)S(1)} %copy.50), channel_id=1, replica_groups=mesh['dom'=128,'rep'=4] {'rep'}, dimensions={0} | all-to-all | bytes 732032 | tf_op jit(solution)/shard_map/all_to_all | solution.py:189
  122.2 1.0 reshape.72.got_ref
  123.2 2.3 %final.1 = f32[300,256]{1,0:T(8,128)} custom-call(bf16[304,602]{1,0:T(8,128)(2,1)} %reshape.72.got_ref), custom_call_target="tpu_custom_call" | custom-call | tf_op jit(solution)/shard_map/final/pallas_call | solution.py:190
  (46 shorter events, 0.9 us)
Async XLA Ops:
  0.0 0.7 copy-start.1
  7.1 19.3 %copy-start.2 = (bf16[32,602]{1,0:T(8,128)(2,1)S(1)}, bf16[32,602]{1,0:T(8,128)(2,1)}, u32[]{:S(2)}) copy-start(bf16[32,602]{1,0:T(8,128)(2,1)} %get-tuple-element.17) | copy-start | bytes 115588
  7.1 44.3 %all-to-all-start = ((bf16[128,2,602]{2,1,0:T(2,128)(2,1)}), bf16[128,2,602]{2,1,0:T(2,128)(2,1)S(1)}, u32[]{:S(2)}, u32[]{:S(2)}) async-start(bf16[128,2,602]{2,1,0:T(2,128)(2,1)} %reshape.64), calls=%async_computation | async-start | bytes 655360 | tf_op jit(solution)/shard_map/all_to_all | solution.py:167
  26.4 13.7 %copy-start = (bf16[512,100]{0,1:T(8,128)(2,1)S(1)}, bf16[512,100]{0,1:T(8,128)(2,1)}, u32[]{:S(2)}) copy-start(bf16[512,100]{0,1:T(8,128)(2,1)} %param.19) | copy-start | bytes 307204
  26.4 18.6 %collective-permute-start = (bf16[3,2,602]{2,1,0:T(2,128)(2,1)S(1)}, bf16[3,2,602]{2,1,0:T(2,128)(2,1)S(1)}, u32[]{:S(2)}, u32[]{:S(2)}) collective-permute-start(bf16[3,2,602]{2,1,0:T(2,128)(2,1)S(1)} %squeeze.31), channel_id=1, source_target_pairs={{0,8},{4,12},{8,16},{12,20},{16,24},{20,28},{24,32},{28,36},{32,40... | collective-permute-start | bytes 21680 | tf_op jit(solution)/shard_map/ppermute | solution.py:123
  29.8 15.3 %collective-permute-start.1 = (bf16[3,2,602]{2,1,0:T(2,128)(2,1)S(1)}, bf16[3,2,602]{2,1,0:T(2,128)(2,1)S(1)}, u32[]{:S(2)}, u32[]{:S(2)}) collective-permute-start(bf16[3,2,602]{2,1,0:T(2,128)(2,1)S(1)} %squeeze.32), channel_id=1, source_target_pairs={{0,4},{4,8},{8,12},{12,16},{16,20},{20,24},{24,28},{28,32},{32,36}... | collective-permute-start | bytes 21680 | tf_op jit(solution)/shard_map/ppermute | solution.py:123
  31.8 13.4 %collective-permute-start.2 = (bf16[3,2,602]{2,1,0:T(2,128)(2,1)S(1)}, bf16[3,2,602]{2,1,0:T(2,128)(2,1)S(1)}, u32[]{:S(2)}, u32[]{:S(2)}) collective-permute-start(bf16[3,2,602]{2,1,0:T(2,128)(2,1)S(1)} %squeeze.34), channel_id=1, source_target_pairs={{0,508},{4,0},{8,4},{12,8},{16,12},{20,16},{24,20},{28,24},{32,28}... | collective-permute-start | bytes 21680 | tf_op jit(solution)/shard_map/ppermute | solution.py:123
  37.6 7.6 %collective-permute-start.3 = (bf16[3,2,602]{2,1,0:T(2,128)(2,1)S(1)}, bf16[3,2,602]{2,1,0:T(2,128)(2,1)S(1)}, u32[]{:S(2)}, u32[]{:S(2)}) collective-permute-start(bf16[3,2,602]{2,1,0:T(2,128)(2,1)S(1)} %squeeze.35), channel_id=1, source_target_pairs={{0,504},{4,508},{8,0},{12,4},{16,8},{20,12},{24,16},{28,20},{32,24... | collective-permute-start | bytes 21680 | tf_op jit(solution)/shard_map/ppermute | solution.py:123
  59.9 28.2 %collective-permute-start.4 = (bf16[3,2,602]{2,1,0:T(2,128)(2,1)S(1)}, bf16[3,2,602]{2,1,0:T(2,128)(2,1)S(1)}, u32[]{:S(2)}, u32[]{:S(2)}) collective-permute-start(bf16[3,2,602]{2,1,0:T(2,128)(2,1)S(1)} %squeeze.36), channel_id=1, source_target_pairs={{0,8},{4,12},{8,16},{12,20},{16,24},{20,28},{24,32},{28,36},{32,40... | collective-permute-start | bytes 21680 | tf_op jit(solution)/shard_map/ppermute | solution.py:123
  62.5 25.7 %collective-permute-start.5 = (bf16[3,2,602]{2,1,0:T(2,128)(2,1)S(1)}, bf16[3,2,602]{2,1,0:T(2,128)(2,1)S(1)}, u32[]{:S(2)}, u32[]{:S(2)}) collective-permute-start(bf16[3,2,602]{2,1,0:T(2,128)(2,1)S(1)} %squeeze.37), channel_id=1, source_target_pairs={{0,4},{4,8},{8,12},{12,16},{16,20},{20,24},{24,28},{28,32},{32,36}... | collective-permute-start | bytes 21680 | tf_op jit(solution)/shard_map/ppermute | solution.py:123
  64.5 23.7 %collective-permute-start.6 = (bf16[3,2,602]{2,1,0:T(2,128)(2,1)S(1)}, bf16[3,2,602]{2,1,0:T(2,128)(2,1)S(1)}, u32[]{:S(2)}, u32[]{:S(2)}) collective-permute-start(bf16[3,2,602]{2,1,0:T(2,128)(2,1)S(1)} %squeeze.38), channel_id=1, source_target_pairs={{0,508},{4,0},{8,4},{12,8},{16,12},{20,16},{24,20},{28,24},{32,28}... | collective-permute-start | bytes 21680 | tf_op jit(solution)/shard_map/ppermute | solution.py:123
  72.1 36.5 %all-to-all-start.1 = ((bf16[128,2,602]{2,1,0:T(2,128)(2,1)}), bf16[128,2,602]{2,1,0:T(2,128)(2,1)S(1)}, u32[]{:S(2)}, u32[]{:S(2)}) async-start(bf16[128,2,602]{2,1,0:T(2,128)(2,1)} %reshape.70), calls=%async_computation.1 | async-start | bytes 655360 | tf_op jit(solution)/shard_map/all_to_all | solution.py:182
  83.6 12.5 %collective-permute-start.7 = (bf16[3,2,602]{2,1,0:T(2,128)(2,1)S(1)}, bf16[3,2,602]{2,1,0:T(2,128)(2,1)S(1)}, u32[]{:S(2)}, u32[]{:S(2)}) collective-permute-start(bf16[3,2,602]{2,1,0:T(2,128)(2,1)S(1)} %squeeze.39), channel_id=1, source_target_pairs={{0,504},{4,508},{8,0},{12,4},{16,8},{20,12},{24,16},{28,20},{32,24... | collective-permute-start | bytes 21680 | tf_op jit(solution)/shard_map/ppermute | solution.py:123

commit v2 on v1

v2 whole, which is shorter than its diff:
```python
import jax
import jax.numpy as jnp
from jax import lax
from jax.experimental import pallas as pl
from jax.experimental.pallas import tpu as pltpu
from jax.sharding import PartitionSpec as P


F32 = jnp.float32
BF16 = jnp.bfloat16
N_DOM = 128
N_REP = 4
CAP = 16
FAR = 4
REACH = 2
FEAT = 300
WIDE = FEAT + 1
PAIR = 2 * WIDE
FAR_ROWS = N_DOM * FAR // 2
NEAR_ROWS = (CAP - FAR) // 2
NEAR_PAD = 32
ROWS = FAR_ROWS + NEAR_PAD
QUARTER = 256
COLS = 1024


def dot(a, b, ca, cb):
    return lax.dot_general(a, b, (((ca,), (cb,)), ((), ())), preferred_element_type=F32)


def pack_kernel(dom_ref, lists_ref, prof_ref, far_ref, near_ref, idx_ref):
    idx = lists_ref[...].T
    idx_ref[...] = idx
    pairs = jnp.broadcast_to(idx[:, None, :], (N_DOM, FAR // 2, CAP)).reshape(FAR_ROWS, CAP)
    first = lax.broadcasted_iota(jnp.int32, (FAR_ROWS, 1), 0) % 2 == 0
    row = lax.broadcasted_iota(jnp.int32, (NEAR_PAD, CAP), 0)
    slot = lax.broadcasted_iota(jnp.int32, (NEAR_PAD, CAP), 1)
    around = jnp.zeros((NEAR_PAD, CAP), jnp.int32)
    for i in range(2 * REACH + 1):
        other = idx_ref[pl.ds((dom_ref[0] + i + N_DOM - REACH) % N_DOM, 1), :]
        around = jnp.where(row // NEAR_ROWS == i, other, around)
    around = around.astype(F32)
    prof = prof_ref[...]
    lane = lax.broadcasted_iota(jnp.int32, (ROWS, COLS), 1)
    halves = []
    for p in range(2):
        near_col = jnp.sum(
            jnp.where(slot == FAR + 2 * (row % NEAR_ROWS) + p, around, 0.0), axis=1, keepdims=True
        ).astype(jnp.int32)
        far_col = jnp.where(first, pairs[:, p : p + 1], pairs[:, 2 + p : 3 + p])
        col = jnp.concatenate([far_col, near_col], axis=0)
        pick = jnp.where(col == lane, 1.0, 0.0).astype(BF16)
        halves.append(dot(pick, prof, 1, 1))
        halves.append((col % QUARTER).astype(F32))
    rows = jnp.concatenate(halves, axis=1).astype(BF16)
    far_ref[...] = rows[:FAR_ROWS].reshape(far_ref.shape)
    near_ref[...] = rows[FAR_ROWS:].reshape(near_ref.shape)


def prep_kernel(
    dom_ref, slot_ref, weight_ref, dep_ref, w_in_ref, w_mid_ref, w_out_ref,
    hi_ref, lo_ref, hi_t_ref, lo_t_ref, seed_ref, w_in_t_ref, w_mid_t_ref,
):
    slot = slot_ref[...]
    owner = slot // CAP
    j = slot % CAP
    apart = (owner - dom_ref[0] + REACH) % N_DOM
    row = jnp.where(
        j < FAR, owner * (FAR // 2) + j // 2, FAR_ROWS + apart * NEAR_ROWS + (j - FAR) // 2
    )
    row = row + ROWS * (j % 2)
    index = lax.broadcasted_iota(jnp.int32, (2 * ROWS, slot.shape[1]), 0)
    acc = jnp.zeros(index.shape, F32)
    for k in range(4):
        acc = acc + jnp.where(row[k : k + 1] == index, weight_ref[k : k + 1], 0.0)
    hi = acc.astype(BF16)
    lo = acc - hi.astype(F32)
    hi_ref[...] = hi
    lo_ref[...] = lo.astype(BF16)
    hi_t_ref[...] = acc.T.astype(BF16)
    lo_t_ref[...] = lo.T.astype(BF16)
    seed_ref[...] = dot(dep_ref[...].astype(BF16), w_out_ref[...], 0, 0)
    w_in_t_ref[...] = w_in_ref[...].T
    w_mid_t_ref[...] = w_mid_ref[...].T


def main_kernel(
    far_ref, near_ref, hi_ref, lo_ref, hi_t_ref, lo_t_ref, seed_ref,
    w_in_ref, b_in_ref, w_mid_ref, b_mid_ref, w_in_t_ref, w_mid_t_ref,
    far_out_ref, near_out_ref,
):
    fetched = jnp.concatenate(
        [far_ref[...].reshape(FAR_ROWS, PAIR), near_ref[...].reshape(NEAR_PAD, PAIR)], axis=0
    )
    values = jnp.concatenate([fetched[:, :FEAT], fetched[:, WIDE : WIDE + FEAT]], axis=0)
    inputs = (dot(hi_t_ref[...], values, 1, 0) + dot(lo_t_ref[...], values, 1, 0)).astype(BF16)
    t_one = jnp.tanh(dot(inputs, w_in_ref[...], 1, 0) + b_in_ref[...])
    t_two = jnp.tanh(dot(t_one.astype(BF16), w_mid_ref[...], 1, 0) + b_mid_ref[...])
    g_two = (seed_ref[...] * (1.0 - t_two * t_two)).astype(BF16)
    g_one = (dot(g_two, w_mid_t_ref[...], 1, 0) * (1.0 - t_one * t_one)).astype(BF16)
    g_inputs = dot(g_one, w_in_t_ref[...], 1, 0)
    g_hi = g_inputs.astype(BF16)
    g_lo = (g_inputs - g_hi.astype(F32)).astype(BF16)
    slots = dot(hi_ref[...], g_hi, 1, 0) + dot(lo_ref[...], g_hi, 1, 0) + dot(hi_ref[...], g_lo, 1, 0)
    rows = jnp.concatenate(
        [
            slots[:ROWS], fetched[:, FEAT:WIDE].astype(F32),
            slots[ROWS:], fetched[:, WIDE + FEAT :].astype(F32),
        ],
        axis=1,
    ).astype(BF16)
    far_out_ref[...] = rows[:FAR_ROWS].reshape(far_out_ref.shape)
    near_out_ref[...] = rows[FAR_ROWS:].reshape(near_out_ref.shape)


def final_kernel(got_ref, out_ref):
    got = got_ref[...].reshape(-1, PAIR)
    lane = lax.broadcasted_iota(jnp.int32, (got.shape[0], QUARTER), 1).astype(F32)
    total = None
    for p in range(2):
        place = got[:, p * WIDE + FEAT : (p + 1) * WIDE].astype(F32)
        pick = jnp.where(place == lane, 1.0, 0.0).astype(BF16)
        part = dot(got[:, p * WIDE : p * WIDE + FEAT], pick, 0, 0)
        total = part if total is None else total + part
    out_ref[...] = total


def shape(dims, dtype):
    return jax.ShapeDtypeStruct(dims, dtype)


def exchange_near(near):
    moved = []
    for i in range(2 * REACH + 1):
        block = near[i * NEAR_ROWS // 2 : (i + 1) * NEAR_ROWS // 2]
        if i != REACH:
            step = i - REACH
            block = lax.ppermute(block, "dom", [(a, (a + step) % N_DOM) for a in range(N_DOM)])
        moved.append(block)
    return moved


def body(
    profiles, pack_index, obs_slot, interp_weight, departures, w_in, b_in, w_mid, b_mid, w_out
):
    dom = lax.axis_index("dom")
    dom_scalar = dom.reshape(1).astype(jnp.int32)
    smem = pl.BlockSpec(memory_space=pltpu.SMEM)
    vmem = pl.BlockSpec(memory_space=pltpu.VMEM)
    far_shape = shape((N_DOM, FAR // 2, PAIR), BF16)
    near_shape = shape((NEAR_PAD // 2, 2, PAIR), BF16)
    far, near = pl.pallas_call(
        pack_kernel,
        out_shape=(far_shape, near_shape),
        in_specs=[smem, vmem, vmem],
        scratch_shapes=[pltpu.VMEM((N_DOM, CAP), jnp.int32)],
        name="pack",
    )(dom_scalar, pack_index[0, 0].T, profiles)

    obs = obs_slot.shape[1]
    hidden = w_mid.shape[0]
    hi, lo, hi_t, lo_t, seed, w_in_t, w_mid_t = pl.pallas_call(
        prep_kernel,
        out_shape=(
            shape((2 * ROWS, obs), BF16), shape((2 * ROWS, obs), BF16),
            shape((obs, 2 * ROWS), BF16), shape((obs, 2 * ROWS), BF16),
            shape((obs, hidden), F32), shape((hidden, FEAT), BF16), shape((hidden, hidden), BF16),
        ),
        in_specs=[smem] + [vmem] * 6,
        name="prep",
    )(dom_scalar, obs_slot, interp_weight, departures, w_in, w_mid, w_out.T)

    got_far = lax.all_to_all(far, "dom", 0, 0, tiled=True)
    got_near = exchange_near(near)
    near_rows = jnp.concatenate(got_near[::-1] + [got_near[REACH][:1]], axis=0)

    far_adj, near_adj = pl.pallas_call(
        main_kernel, out_shape=(far_shape, near_shape), name="main"
    )(
        got_far, near_rows, hi, lo, hi_t, lo_t, seed,
        w_in, b_in.reshape(1, -1), w_mid, b_mid.reshape(1, -1), w_in_t, w_mid_t,
    )

    back_far = lax.all_to_all(far_adj, "dom", 0, 0, tiled=True)
    back_near = exchange_near(near_adj)[::-1]
    stacked = jnp.stack(back_near[:N_REP] * 2)
    first = lax.dynamic_slice_in_dim(stacked, (REACH - dom) % N_REP, N_REP, 0)
    owner = (jnp.arange(N_REP) == (dom + REACH) % N_REP).reshape(N_REP, 1, 1, 1)
    second = jnp.where(owner, back_near[N_REP][None], jnp.zeros((), BF16))
    by_quarter = back_far.reshape(N_DOM // N_REP, N_REP, FAR // 2, PAIR).transpose(1, 0, 2, 3)
    outgoing = jnp.concatenate([by_quarter, first, second], axis=1)
    got = lax.all_to_all(outgoing, "rep", 0, 0, tiled=True)
    return pl.pallas_call(
        final_kernel, out_shape=shape((FEAT, QUARTER), F32), name="final"
    )(got)


def solution(mesh):
    placed = (
        P(None, "dom"),
        P("dom", "rep", None, None),
        P(None, ("dom", "rep")),
        P(None, ("dom", "rep")),
        P(None, ("dom", "rep")),
        P(),
        P(),
        P(),
        P(),
        P(),
    )
    return jax.shard_map(
        body, mesh=mesh, in_specs=placed, out_specs=P(None, ("dom", "rep")), check_vma=False
    )
```

time: 126 us -> 127 us (level)
  local copies, waits for them, and re-layouts: 9.94 us -> 3.36 us
  waiting for transfers between devices: 25.7 us -> 30.6 us
  starting transfers between devices: 59 us -> 62.6 us
    ppermute x8, waiting for transfers between devices: 7.7 us -> 15.8 us  [exchange_near(): lax.ppermute(block, 'dom', [(a, (a + step) % N_DOM) for a in range(N_DOM)])]
    all_to_all x2, starting transfers between devices: 30.7 us -> 38.7 us  [the longest x1 19.4 us: body(): back_far = lax.all_to_all(far_adj, 'dom', 0, 0, tiled=True)]
    reshape x7 -> x1, local copies, waits for them, and re-layouts: 5.93 us -> 0.23 us  [body(): back_far.reshape(N_DOM // N_REP, N_REP, FAR // 2, PAIR)]
    ppermute x8, starting transfers between devices: 28.3 us -> 23.9 us  [exchange_near(): lax.ppermute(block, 'dom', [(a, (a + step) % N_DOM) for a in range(N_DOM)])]
    all_to_all x2, waiting for transfers between devices: 18 us -> 14.8 us  [the longest x1 12.4 us: body(): back_far = lax.all_to_all(far_adj, 'dom', 0, 0, tiled=True)]
  transfers between devices with their start and end apart: 10 -> 10, of which waited for: 3 -> 5; matrix products, arithmetic and copies ran while one was open for 3% -> 1% of each run, Pallas kernels for 3% -> 3%
where the time goes in v2:
time: 127 us
  starting transfers between devices  62.6 us (49%)
  waiting for transfers between devices  30.6 us (24%)
  Pallas kernels  16.4 us (13%)
  blocking collectives  12.8 us (10%)
  local copies, waits for them, and re-layouts  3.36 us (3%)
    ppermute x8, starting transfers between devices, exchange_near(): lax.ppermute(block, 'dom', [(a, (a + step) % N_DOM) for a in range(N_DOM)])  23.9 us
    all_to_all x1, starting transfers between devices, body(): back_far = lax.all_to_all(far_adj, 'dom', 0, 0, tiled=True)  19.4 us
    all_to_all x1, starting transfers between devices, body(): got_far = lax.all_to_all(far, 'dom', 0, 0, tiled=True)  19.3 us
    ppermute x8, waiting for transfers between devices, exchange_near(): lax.ppermute(block, 'dom', [(a, (a + step) % N_DOM) for a in range(N_DOM)])  15.8 us
    all_to_all x1, blocking collectives, body(): got = lax.all_to_all(outgoing, 'rep', 0, 0, tiled=True)  12.8 us
    all_to_all x1, waiting for transfers between devices, body(): back_far = lax.all_to_all(far_adj, 'dom', 0, 0, tiled=True)  12.4 us
    pallas_call x1, Pallas kernels, body(): pl.pallas_call(main_kernel, out_shape=(far_shape, near_shape), name='main')  6.56 us
    pallas_call x1, Pallas kernels, body(): pl.pallas_call(prep_kernel, out_shape=(shape((2 * ROWS, obs), BF16), shap...  3.94 us
  transfers between devices with their start and end apart: 10, of which 5 were waited for; matrix products, arithmetic and copies ran while one was open for 1% of the time, Pallas kernels for 3%

profile of v2, /device:TPU:32, one launch (start us, length us, event | category | flops | bytes accessed | tf_op | source)
XLA Modules:
  0.0 126.6 jit_solution(2668649863539255773)
XLA Ops:
  0.0 3.0 %pack.1 = (bf16[128,2,602]{2,1,0:T(2,128)(2,1)}, bf16[16,2,602]{2,1,0:T(2,128)(2,1)}) custom-call(s32[1]{0:T(128)} %bitcast.dom_ref, s32[16,128]{1,0:T(8,128)} %bitcast.26, bf16[300,1024]{1,0:T(8,128)(2,1)} %prof_ref.1), custom_call_target="tpu_custom_call" | custom-call | tf_op jit(solution)/shard_map/pack/pallas_call | solution.py:152
  3.0 19.3 %all-to-all-start = ((bf16[128,2,602]{2,1,0:T(2,128)(2,1)}), bf16[128,2,602]{2,1,0:T(2,128)(2,1)S(1)}, u32[]{:S(2)}, u32[]{:S(2)}) async-start(bf16[128,2,602]{2,1,0:T(2,128)(2,1)} %get-tuple-element.16), calls=%async_computation | async-start | bytes 655360 | tf_op jit(solution)/shard_map/all_to_all | solution.py:173
  22.4 3.4 %collective-permute-start = (bf16[3,2,602]{2,1,0:T(2,128)(2,1)S(1)}, bf16[3,2,602]{2,1,0:T(2,128)(2,1)S(1)}, u32[]{:S(2)}, u32[]{:S(2)}) collective-permute-start(bf16[3,2,602]{2,1,0:T(2,128)(2,1)S(1)} %get-tuple-element.35), channel_id=1, source_target_pairs={{0,8},{4,12},{8,16},{12,20},{16,24},{20,28},{24,32},{28,36},{32,40... | collective-permute-start | bytes 21680 | tf_op jit(solution)/shard_map/ppermute | solution.py:138
  25.8 1.9 %collective-permute-start.1 = (bf16[3,2,602]{2,1,0:T(2,128)(2,1)S(1)}, bf16[3,2,602]{2,1,0:T(2,128)(2,1)S(1)}, u32[]{:S(2)}, u32[]{:S(2)}) collective-permute-start(bf16[3,2,602]{2,1,0:T(2,128)(2,1)S(1)} %get-tuple-element.34), channel_id=1, source_target_pairs={{0,4},{4,8},{8,12},{12,16},{16,20},{20,24},{24,28},{28,32},{32,36}... | collective-permute-start | bytes 21680 | tf_op jit(solution)/shard_map/ppermute | solution.py:138
  27.7 5.8 %collective-permute-done = bf16[3,2,602]{2,1,0:T(2,128)(2,1)S(1)} collective-permute-done((bf16[3,2,602]{2,1,0:T(2,128)(2,1)S(1)}, bf16[3,2,602]{2,1,0:T(2,128)(2,1)S(1)}, u32[]{:S(2)}, u32[]{:S(2)}) %collective-permute-start) | collective-permute-done | bytes 7256 | tf_op jit(solution)/shard_map/ppermute | solution.py:138
  33.5 0.0 collective-permute-done.1
  33.6 1.9 %collective-permute-start.2 = (bf16[3,2,602]{2,1,0:T(2,128)(2,1)S(1)}, bf16[3,2,602]{2,1,0:T(2,128)(2,1)S(1)}, u32[]{:S(2)}, u32[]{:S(2)}) collective-permute-start(bf16[3,2,602]{2,1,0:T(2,128)(2,1)S(1)} %get-tuple-element.32), channel_id=1, source_target_pairs={{0,508},{4,0},{8,4},{12,8},{16,12},{20,16},{24,20},{28,24},{32,28}... | collective-permute-start | bytes 21680 | tf_op jit(solution)/shard_map/ppermute | solution.py:138
  35.6 3.9 %prep.1 = (bf16[576,512]{1,0:T(8,128)(2,1)}, bf16[576,512]{1,0:T(8,128)(2,1)}, bf16[512,576]{1,0:T(8,128)(2,1)}, bf16[512,576]{1,0:T(8,128)(2,1)}, f32[512,512]{...) custom-call(s32[1]{0:T(128)} %bitcast.dom_ref, s32[4,512]{1,0:T(4,128)} %slot_ref.1, ...), custom_call_target="tpu_custom_call" | custom-call | tf_op jit(solution)/shard_map/prep/pallas_call | solution.py:162
  39.5 1.9 %collective-permute-start.3 = (bf16[3,2,602]{2,1,0:T(2,128)(2,1)S(1)}, bf16[3,2,602]{2,1,0:T(2,128)(2,1)S(1)}, u32[]{:S(2)}, u32[]{:S(2)}) collective-permute-start(bf16[3,2,602]{2,1,0:T(2,128)(2,1)S(1)} %get-tuple-element.31), channel_id=1, source_target_pairs={{0,504},{4,508},{8,0},{12,4},{16,8},{20,12},{24,16},{28,20},{32,24... | collective-permute-start | bytes 21680 | tf_op jit(solution)/shard_map/ppermute | solution.py:138
  41.4 0.0 collective-permute-done.2
  41.5 3.6 %collective-permute-done.3 = bf16[3,2,602]{2,1,0:T(2,128)(2,1)S(1)} collective-permute-done((bf16[3,2,602]{2,1,0:T(2,128)(2,1)S(1)}, bf16[3,2,602]{2,1,0:T(2,128)(2,1)S(1)}, u32[]{:S(2)}, u32[]{:S(2)}) %collective-permute-start.3) | collective-permute-done | bytes 7256 | tf_op jit(solution)/shard_map/ppermute | solution.py:138
  45.1 0.0 copy-start.1
  45.1 2.3 %all-to-all-done.far_ref = bf16[128,2,602]{2,1,0:T(2,128)(2,1)S(1)} async-done(((bf16[128,2,602]{2,1,0:T(2,128)(2,1)}), bf16[128,2,602]{2,1,0:T(2,128)(2,1)S(1)}, u32[]{:S(2)}, u32[]{:S(2)}) %all-to-all-start) | async-done | bytes 308256 | tf_op jit(solution)/shard_map/all_to_all | solution.py:173
  47.4 0.7 copy-done
  48.1 6.6 %main.1 = (bf16[128,2,602]{2,1,0:T(2,128)(2,1)}, bf16[16,2,602]{2,1,0:T(2,128)(2,1)}) custom-call(bf16[128,2,602]{2,1,0:T(2,128)(2,1)} %copy-done, bf16[16,2,602]{2,1,0:T(2,128)(2,1)} %copy-done.1, bf16[576,512]{1,0:T(8,128)(2,1)} %get-tuple-element.18.hi_ref, bf16[576,512]{1,0:T(8,128)(2,1)} %get-tuple-element.19.lo_ref, ...), custom_call_target="tpu_custom_call" | custom-call | tf_op jit(solution)/shard_map/main/pallas_call | solution.py:177
  54.7 0.8 fusion
  55.5 2.5 %collective-permute-start.4 = (bf16[3,2,602]{2,1,0:T(2,128)(2,1)S(1)}, bf16[3,2,602]{2,1,0:T(2,128)(2,1)S(1)}, u32[]{:S(2)}, u32[]{:S(2)}) collective-permute-start(bf16[3,2,602]{2,1,0:T(2,128)(2,1)S(1)} %get-tuple-element.30), channel_id=1, source_target_pairs={{0,8},{4,12},{8,16},{12,20},{16,24},{20,28},{24,32},{28,36},{32,40... | collective-permute-start | bytes 21680 | tf_op jit(solution)/shard_map/ppermute | solution.py:138
  58.0 1.9 %collective-permute-start.5 = (bf16[3,2,602]{2,1,0:T(2,128)(2,1)S(1)}, bf16[3,2,602]{2,1,0:T(2,128)(2,1)S(1)}, u32[]{:S(2)}, u32[]{:S(2)}) collective-permute-start(bf16[3,2,602]{2,1,0:T(2,128)(2,1)S(1)} %get-tuple-element.29), channel_id=1, source_target_pairs={{0,4},{4,8},{8,12},{12,16},{16,20},{20,24},{24,28},{28,32},{32,36}... | collective-permute-start | bytes 21680 | tf_op jit(solution)/shard_map/ppermute | solution.py:138
  60.0 5.8 %collective-permute-start.6 = (bf16[3,2,602]{2,1,0:T(2,128)(2,1)S(1)}, bf16[3,2,602]{2,1,0:T(2,128)(2,1)S(1)}, u32[]{:S(2)}, u32[]{:S(2)}) collective-permute-start(bf16[3,2,602]{2,1,0:T(2,128)(2,1)S(1)} %get-tuple-element.27), channel_id=1, source_target_pairs={{0,508},{4,0},{8,4},{12,8},{16,12},{20,16},{24,20},{28,24},{32,28}... | collective-permute-start | bytes 21680 | tf_op jit(solution)/shard_map/ppermute | solution.py:138
  65.7 19.4 %all-to-all-start.1 = ((bf16[128,2,602]{2,1,0:T(2,128)(2,1)}), bf16[128,2,602]{2,1,0:T(2,128)(2,1)S(1)}, u32[]{:S(2)}, u32[]{:S(2)}) async-start(bf16[128,2,602]{2,1,0:T(2,128)(2,1)} %get-tuple-element.25), calls=%async_computation.1 | async-start | bytes 655360 | tf_op jit(solution)/shard_map/all_to_all | solution.py:184
  85.1 4.6 %collective-permute-start.7 = (bf16[3,2,602]{2,1,0:T(2,128)(2,1)S(1)}, bf16[3,2,602]{2,1,0:T(2,128)(2,1)S(1)}, u32[]{:S(2)}, u32[]{:S(2)}) collective-permute-start(bf16[3,2,602]{2,1,0:T(2,128)(2,1)S(1)} %get-tuple-element.28), channel_id=1, source_target_pairs={{0,504},{4,508},{8,0},{12,4},{16,8},{20,12},{24,16},{28,20},{32,24... | collective-permute-start | bytes 21680 | tf_op jit(solution)/shard_map/ppermute | solution.py:138
  89.7 0.0 collective-permute-done.4
  89.7 0.7 constant_dynamic-update-slice_fusion.11
  90.4 0.0 collective-permute-done.6
  90.5 0.7 constant_dynamic-update-slice_fusion.7
  91.3 6.3 %collective-permute-done.7 = bf16[3,2,602]{2,1,0:T(2,128)(2,1)S(1)} collective-permute-done((bf16[3,2,602]{2,1,0:T(2,128)(2,1)S(1)}, bf16[3,2,602]{2,1,0:T(2,128)(2,1)S(1)}, u32[]{:S(2)}, u32[]{:S(2)}) %collective-permute-start.7) | collective-permute-done | bytes 7256 | tf_op jit(solution)/shard_map/ppermute | solution.py:138
  97.6 0.1 broadcast_select_fusion
  97.7 12.4 %all-to-all-done.1 = bf16[128,2,602]{2,1,0:T(2,128)(2,1)S(1)} async-done(((bf16[128,2,602]{2,1,0:T(2,128)(2,1)}), bf16[128,2,602]{2,1,0:T(2,128)(2,1)S(1)}, u32[]{:S(2)}, u32[]{:S(2)}) %all-to-all-start.1) | async-done | bytes 308256 | tf_op jit(solution)/shard_map/all_to_all | solution.py:184
  110.1 0.2 copy.13
  110.4 0.6 pad_maximum_fusion
  110.9 12.8 %all_to_all.15.got_ref = bf16[4,38,2,602]{3,2,1,0:T(2,128)(2,1)} all-to-all(bf16[4,38,2,602]{3,2,1,0:T(2,128)(2,1)S(1)} %pad_maximum_fusion), channel_id=1, replica_groups=mesh['dom'=128,'rep'=4] {'rep'}, dimensions={0} | all-to-all | bytes 732032 | tf_op jit(solution)/shard_map/all_to_all | solution.py:192
  123.8 2.8 %final.1 = f32[300,256]{1,0:T(8,128)} custom-call(bf16[4,38,2,602]{3,2,1,0:T(2,128)(2,1)} %all_to_all.15.got_ref), custom_call_target="tpu_custom_call" | custom-call | tf_op jit(solution)/shard_map/final/pallas_call | solution.py:193
  (20 shorter events, 0.2 us)
Async XLA Ops:
  3.0 19.3 %copy-start.2 = (bf16[16,2,602]{2,1,0:T(2,128)(2,1)S(1)}, bf16[16,2,602]{2,1,0:T(2,128)(2,1)}, u32[]{:S(2)}) copy-start(bf16[16,2,602]{2,1,0:T(2,128)(2,1)} %get-tuple-element.17) | copy-start | bytes 115588
  3.0 44.4 %all-to-all-start = ((bf16[128,2,602]{2,1,0:T(2,128)(2,1)}), bf16[128,2,602]{2,1,0:T(2,128)(2,1)S(1)}, u32[]{:S(2)}, u32[]{:S(2)}) async-start(bf16[128,2,602]{2,1,0:T(2,128)(2,1)} %get-tuple-element.16), calls=%async_computation | async-start | bytes 655360 | tf_op jit(solution)/shard_map/all_to_all | solution.py:173
  22.4 11.1 %collective-permute-start = (bf16[3,2,602]{2,1,0:T(2,128)(2,1)S(1)}, bf16[3,2,602]{2,1,0:T(2,128)(2,1)S(1)}, u32[]{:S(2)}, u32[]{:S(2)}) collective-permute-start(bf16[3,2,602]{2,1,0:T(2,128)(2,1)S(1)} %get-tuple-element.35), channel_id=1, source_target_pairs={{0,8},{4,12},{8,16},{12,20},{16,24},{20,28},{24,32},{28,36},{32,40... | collective-permute-start | bytes 21680 | tf_op jit(solution)/shard_map/ppermute | solution.py:138
  25.8 7.8 %collective-permute-start.1 = (bf16[3,2,602]{2,1,0:T(2,128)(2,1)S(1)}, bf16[3,2,602]{2,1,0:T(2,128)(2,1)S(1)}, u32[]{:S(2)}, u32[]{:S(2)}) collective-permute-start(bf16[3,2,602]{2,1,0:T(2,128)(2,1)S(1)} %get-tuple-element.34), channel_id=1, source_target_pairs={{0,4},{4,8},{8,12},{12,16},{16,20},{20,24},{24,28},{28,32},{32,36}... | collective-permute-start | bytes 21680 | tf_op jit(solution)/shard_map/ppermute | solution.py:138
  33.6 7.8 %collective-permute-start.2 = (bf16[3,2,602]{2,1,0:T(2,128)(2,1)S(1)}, bf16[3,2,602]{2,1,0:T(2,128)(2,1)S(1)}, u32[]{:S(2)}, u32[]{:S(2)}) collective-permute-start(bf16[3,2,602]{2,1,0:T(2,128)(2,1)S(1)} %get-tuple-element.32), channel_id=1, source_target_pairs={{0,508},{4,0},{8,4},{12,8},{16,12},{20,16},{24,20},{28,24},{32,28}... | collective-permute-start | bytes 21680 | tf_op jit(solution)/shard_map/ppermute | solution.py:138
  39.5 5.5 %collective-permute-start.3 = (bf16[3,2,602]{2,1,0:T(2,128)(2,1)S(1)}, bf16[3,2,602]{2,1,0:T(2,128)(2,1)S(1)}, u32[]{:S(2)}, u32[]{:S(2)}) collective-permute-start(bf16[3,2,602]{2,1,0:T(2,128)(2,1)S(1)} %get-tuple-element.31), channel_id=1, source_target_pairs={{0,504},{4,508},{8,0},{12,4},{16,8},{20,12},{24,16},{28,20},{32,24... | collective-permute-start | bytes 21680 | tf_op jit(solution)/shard_map/ppermute | solution.py:138
  45.1 2.3 %copy-start.1 = (bf16[16,2,602]{2,1,0:T(2,128)(2,1)}, bf16[16,2,602]{2,1,0:T(2,128)(2,1)S(1)}, u32[]{:S(2)}) copy-start(bf16[16,2,602]{2,1,0:T(2,128)(2,1)S(1)} %constant_dynamic-update-slice_fusion.near_ref) | copy-start | bytes 115588
  47.4 0.7 copy-start
  55.5 34.2 %collective-permute-start.4 = (bf16[3,2,602]{2,1,0:T(2,128)(2,1)S(1)}, bf16[3,2,602]{2,1,0:T(2,128)(2,1)S(1)}, u32[]{:S(2)}, u32[]{:S(2)}) collective-permute-start(bf16[3,2,602]{2,1,0:T(2,128)(2,1)S(1)} %get-tuple-element.30), channel_id=1, source_target_pairs={{0,8},{4,12},{8,16},{12,20},{16,24},{20,28},{24,32},{28,36},{32,40... | collective-permute-start | bytes 21680 | tf_op jit(solution)/shard_map/ppermute | solution.py:138
  58.0 31.7 %collective-permute-start.5 = (bf16[3,2,602]{2,1,0:T(2,128)(2,1)S(1)}, bf16[3,2,602]{2,1,0:T(2,128)(2,1)S(1)}, u32[]{:S(2)}, u32[]{:S(2)}) collective-permute-start(bf16[3,2,602]{2,1,0:T(2,128)(2,1)S(1)} %get-tuple-element.29), channel_id=1, source_target_pairs={{0,4},{4,8},{8,12},{12,16},{16,20},{20,24},{24,28},{28,32},{32,36}... | collective-permute-start | bytes 21680 | tf_op jit(solution)/shard_map/ppermute | solution.py:138
  60.0 30.5 %collective-permute-start.6 = (bf16[3,2,602]{2,1,0:T(2,128)(2,1)S(1)}, bf16[3,2,602]{2,1,0:T(2,128)(2,1)S(1)}, u32[]{:S(2)}, u32[]{:S(2)}) collective-permute-start(bf16[3,2,602]{2,1,0:T(2,128)(2,1)S(1)} %get-tuple-element.27), channel_id=1, source_target_pairs={{0,508},{4,0},{8,4},{12,8},{16,12},{20,16},{24,20},{28,24},{32,28}... | collective-permute-start | bytes 21680 | tf_op jit(solution)/shard_map/ppermute | solution.py:138
  65.7 44.4 %all-to-all-start.1 = ((bf16[128,2,602]{2,1,0:T(2,128)(2,1)}), bf16[128,2,602]{2,1,0:T(2,128)(2,1)S(1)}, u32[]{:S(2)}, u32[]{:S(2)}) async-start(bf16[128,2,602]{2,1,0:T(2,128)(2,1)} %get-tuple-element.25), calls=%async_computation.1 | async-start | bytes 655360 | tf_op jit(solution)/shard_map/all_to_all | solution.py:184
  85.1 12.5 %collective-permute-start.7 = (bf16[3,2,602]{2,1,0:T(2,128)(2,1)S(1)}, bf16[3,2,602]{2,1,0:T(2,128)(2,1)S(1)}, u32[]{:S(2)}, u32[]{:S(2)}) collective-permute-start(bf16[3,2,602]{2,1,0:T(2,128)(2,1)S(1)} %get-tuple-element.28), channel_id=1, source_target_pairs={{0,504},{4,508},{8,0},{12,4},{16,8},{20,12},{24,16},{28,20},{32,24... | collective-permute-start | bytes 21680 | tf_op jit(solution)/shard_map/ppermute | solution.py:138

commit v3 on v2

v3 whole, which is shorter than its diff:
```python
import jax
import jax.numpy as jnp
from jax import lax
from jax.experimental import pallas as pl
from jax.experimental.pallas import tpu as pltpu
from jax.sharding import PartitionSpec as P


F32 = jnp.float32
BF16 = jnp.bfloat16
N_DOM = 128
N_REP = 4
CAP = 16
FAR = 4
REACH = 2
FEAT = 300
WIDE = FEAT + 1
PAIR = 2 * WIDE
FAR_ROWS = N_DOM * FAR // 2
NEAR_ROWS = (CAP - FAR) // 2
NEAR_STEP = 8
NEAR_PAD = 48
BLOCKS = 2 * REACH + 1
ROWS = FAR_ROWS + NEAR_PAD
QUARTER = 256
COLS = 1024
KERNEL_VMEM = 24 * 2**20
N_HELD = 2
N_NEARBY = 6


def dot(a, b, ca, cb):
    return lax.dot_general(a, b, (((ca,), (cb,)), ((), ())), preferred_element_type=F32)


def put_near(near_refs, rows):
    for i, ref in enumerate(near_refs):
        start = FAR_ROWS + i * NEAR_STEP
        ref[...] = rows[start : start + NEAR_STEP].reshape(ref.shape)


def pack_kernel(dom_ref, lists_ref, prof_ref, far_ref, *rest):
    near_refs, idx_ref = rest[:BLOCKS], rest[BLOCKS]
    idx = lists_ref[...].T
    idx_ref[...] = idx
    pairs = jnp.broadcast_to(idx[:, None, :], (N_DOM, FAR // 2, CAP)).reshape(FAR_ROWS, CAP)
    first = lax.broadcasted_iota(jnp.int32, (FAR_ROWS, 1), 0) % 2 == 0
    row = lax.broadcasted_iota(jnp.int32, (NEAR_PAD, CAP), 0)
    slot = lax.broadcasted_iota(jnp.int32, (NEAR_PAD, CAP), 1)
    around = jnp.zeros((NEAR_PAD, CAP), jnp.int32)
    for i in range(BLOCKS):
        other = idx_ref[pl.ds((dom_ref[0] + i + N_DOM - REACH) % N_DOM, 1), :]
        around = jnp.where(row // NEAR_STEP == i, other, around)
    around = around.astype(F32)
    prof = prof_ref[...]
    lane = lax.broadcasted_iota(jnp.int32, (ROWS, COLS), 1)
    halves = []
    for p in range(2):
        near_col = jnp.sum(
            jnp.where(slot == FAR + 2 * (row % NEAR_STEP) + p, around, 0.0), axis=1, keepdims=True
        ).astype(jnp.int32)
        far_col = jnp.where(first, pairs[:, p : p + 1], pairs[:, 2 + p : 3 + p])
        col = jnp.concatenate([far_col, near_col], axis=0)
        pick = jnp.where(col == lane, 1.0, 0.0).astype(BF16)
        halves.append(dot(pick, prof, 1, 1))
        halves.append((col % QUARTER).astype(F32))
    rows = jnp.concatenate(halves, axis=1).astype(BF16)
    far_ref[...] = rows[:FAR_ROWS].reshape(far_ref.shape)
    put_near(near_refs, rows)


def prep_kernel(
    dom_ref, slot_ref, weight_ref, dep_ref, w_out_ref,
    hi_ref, hi_t_ref, lo_t_ref, seed_ref,
):
    slot = slot_ref[...]
    owner = slot // CAP
    j = slot % CAP
    apart = (owner - dom_ref[0] + REACH) % N_DOM
    row = jnp.where(
        j < FAR, owner * (FAR // 2) + j // 2, FAR_ROWS + apart * NEAR_STEP + (j - FAR) // 2
    )
    row = row + ROWS * (j % 2)
    index = lax.broadcasted_iota(jnp.int32, (2 * ROWS, slot.shape[1]), 0)
    acc = jnp.zeros(index.shape, F32)
    for k in range(4):
        acc = acc + jnp.where(row[k : k + 1] == index, weight_ref[k : k + 1], 0.0)
    hi = acc.astype(BF16)
    lo = acc - hi.astype(F32)
    hi_ref[...] = hi
    hi_t_ref[...] = acc.T.astype(BF16)
    lo_t_ref[...] = lo.T.astype(BF16)
    seed_ref[...] = dot(dep_ref[...].astype(BF16), w_out_ref[...], 0, 0)


def main_kernel(far_ref, *refs):
    near_refs = refs[:BLOCKS]
    refs = refs[BLOCKS:]
    hi_t_ref, lo_t_ref, b_in_ref, b_mid_ref, w_in_ref, w_mid_ref = refs[:N_NEARBY]
    remote, refs = refs[N_NEARBY : N_NEARBY + N_HELD], refs[N_NEARBY + N_HELD :]
    far_out_ref, *near_out_refs = refs[: BLOCKS + 1]
    *held, sems = refs[BLOCKS + 1 :]
    copies = [pltpu.make_async_copy(a, b, sems.at[i]) for i, (a, b) in enumerate(zip(remote, held))]
    for copy in copies:
        copy.start()

    def ready(i):
        copies[i].wait()
        return held[i][...]

    parts = [far_ref[...].reshape(FAR_ROWS, PAIR)]
    parts += [ref[...].reshape(NEAR_STEP, PAIR) for ref in near_refs]
    parts += [jnp.zeros((ROWS - FAR_ROWS - BLOCKS * NEAR_STEP, PAIR), BF16)]
    fetched = jnp.concatenate(parts, axis=0)
    values = jnp.concatenate([fetched[:, :FEAT], fetched[:, WIDE : WIDE + FEAT]], axis=0)
    inputs = (dot(hi_t_ref[...], values, 1, 0) + dot(lo_t_ref[...], values, 1, 0)).astype(BF16)
    w_in = w_in_ref[...]
    t_one = jnp.tanh(dot(inputs, w_in, 1, 0) + b_in_ref[...])
    w_mid = w_mid_ref[...]
    t_two = jnp.tanh(dot(t_one.astype(BF16), w_mid, 1, 0) + b_mid_ref[...])
    g_two = (ready(0) * (1.0 - t_two * t_two)).astype(BF16)
    g_one = (dot(g_two, w_mid, 1, 1) * (1.0 - t_one * t_one)).astype(BF16)
    g_inputs = dot(g_one, w_in, 1, 1).astype(BF16)
    slots = dot(ready(1), g_inputs, 1, 0)
    rows = jnp.concatenate(
        [
            slots[:ROWS], fetched[:, FEAT:WIDE].astype(F32),
            slots[ROWS:], fetched[:, WIDE + FEAT :].astype(F32),
        ],
        axis=1,
    ).astype(BF16)
    far_out_ref[...] = rows[:FAR_ROWS].reshape(far_out_ref.shape)
    put_near(near_out_refs, rows)


def final_kernel(got_ref, out_ref):
    got = got_ref[...].reshape(-1, PAIR)
    lane = lax.broadcasted_iota(jnp.int32, (got.shape[0], QUARTER), 1).astype(F32)
    total = None
    for p in range(2):
        place = got[:, p * WIDE + FEAT : (p + 1) * WIDE].astype(F32)
        pick = jnp.where(place == lane, 1.0, 0.0).astype(BF16)
        part = dot(got[:, p * WIDE : p * WIDE + FEAT], pick, 0, 0)
        total = part if total is None else total + part
    out_ref[...] = total


def shape(dims, dtype):
    return jax.ShapeDtypeStruct(dims, dtype)


def exchange_near(near):
    moved = []
    for i, block in enumerate(near):
        if i != REACH:
            step = i - REACH
            block = lax.ppermute(block, "dom", [(a, (a + step) % N_DOM) for a in range(N_DOM)])
        moved.append(block)
    return moved


def body(
    profiles, pack_index, obs_slot, interp_weight, departures, w_in, b_in, w_mid, b_mid, w_out
):
    dom = lax.axis_index("dom")
    dom_scalar = dom.reshape(1).astype(jnp.int32)
    smem = pl.BlockSpec(memory_space=pltpu.SMEM)
    vmem = pl.BlockSpec(memory_space=pltpu.VMEM)
    far_shape = shape((N_DOM, FAR // 2, PAIR), BF16)
    near_shape = shape((NEAR_STEP // 2, 2, PAIR), BF16)
    far, *near = pl.pallas_call(
        pack_kernel,
        out_shape=(far_shape,) + (near_shape,) * BLOCKS,
        in_specs=[smem, vmem, vmem],
        scratch_shapes=[pltpu.VMEM((N_DOM, CAP), jnp.int32)],
        name="pack",
    )(dom_scalar, pack_index[0, 0].T, profiles)

    obs = obs_slot.shape[1]
    hidden = w_mid.shape[0]
    hi, hi_t, lo_t, seed = pl.pallas_call(
        prep_kernel,
        out_shape=(
            pltpu.HBM((2 * ROWS, obs), BF16), pltpu.VMEM((obs, 2 * ROWS), BF16),
            pltpu.VMEM((obs, 2 * ROWS), BF16), pltpu.HBM((obs, hidden), F32),
        ),
        in_specs=[smem] + [vmem] * 4,
        compiler_params=pltpu.CompilerParams(vmem_limit_bytes=KERNEL_VMEM),
        name="prep",
    )(dom_scalar, obs_slot, interp_weight, departures, w_out.T)

    got_far = lax.all_to_all(far, "dom", 0, 0, tiled=True)
    got_near = exchange_near(near)
    near_by = [pltpu.with_memory_space_constraint(x, pltpu.VMEM) for x in (got_far, hi_t, lo_t)]
    far_away = [pltpu.with_memory_space_constraint(x, pltpu.HBM) for x in (seed, hi)]
    far_adj, *near_adj = pl.pallas_call(
        main_kernel,
        out_shape=(pltpu.HBM(far_shape.shape, BF16),) + (near_shape,) * BLOCKS,
        in_specs=[vmem] * (1 + BLOCKS + N_NEARBY) + [pl.BlockSpec(memory_space=pltpu.HBM)] * N_HELD,
        scratch_shapes=[pltpu.VMEM(x.shape, x.dtype) for x in far_away]
        + [pltpu.SemaphoreType.DMA((N_HELD,))],
        compiler_params=pltpu.CompilerParams(vmem_limit_bytes=KERNEL_VMEM),
        name="main",
    )(
        near_by[0], *got_near[::-1], near_by[1], near_by[2],
        b_in.reshape(1, -1), b_mid.reshape(1, -1), w_in, w_mid, *far_away,
    )

    back_far = lax.all_to_all(far_adj, "dom", 0, 0, tiled=True)
    back_near = [x[: NEAR_ROWS // 2] for x in exchange_near(near_adj)[::-1]]
    stacked = jnp.stack(back_near[:N_REP] * 2)
    first = lax.dynamic_slice_in_dim(stacked, (REACH - dom) % N_REP, N_REP, 0)
    owner = (jnp.arange(N_REP) == (dom + REACH) % N_REP).reshape(N_REP, 1, 1, 1)
    second = jnp.where(owner, back_near[N_REP][None], jnp.zeros((), BF16))
    by_quarter = back_far.reshape(N_DOM // N_REP, N_REP, FAR // 2, PAIR).transpose(1, 0, 2, 3)
    outgoing = jnp.concatenate([by_quarter, first, second], axis=1)
    got = lax.all_to_all(outgoing, "rep", 0, 0, tiled=True)
    return pl.pallas_call(
        final_kernel, out_shape=shape((FEAT, QUARTER), F32), name="final"
    )(got)


def solution(mesh):
    placed = (
        P(None, "dom"),
        P("dom", "rep", None, None),
        P(None, ("dom", "rep")),
        P(None, ("dom", "rep")),
        P(None, ("dom", "rep")),
        P(),
        P(),
        P(),
        P(),
        P(),
    )
    return jax.shard_map(
        body, mesh=mesh, in_specs=placed, out_specs=P(None, ("dom", "rep")), check_vma=False
    )
```

time: 127 us -> 116 us (0.913)
  starting transfers between devices: 62.6 us -> 54.3 us
  Pallas kernels: 16.4 us -> 11.7 us
  waiting for transfers between devices: 30.6 us -> 32.7 us
    ppermute x8, waiting for transfers between devices: 15.8 us -> 0.95 us  [exchange_near(): lax.ppermute(block, 'dom', [(a, (a + step) % N_DOM) for a in range(N_DOM)])]
    all_to_all x1, starting transfers between devices: 19.4 us -> 7.86 us  [body(): back_far = lax.all_to_all(far_adj, 'dom', 0, 0, tiled=True)]
    all_to_all x1, waiting for transfers between devices: 12.4 us -> 23.5 us  [body(): back_far = lax.all_to_all(far_adj, 'dom', 0, 0, tiled=True)]
    all_to_all x1, waiting for transfers between devices: 2.32 us -> 8.25 us  [body(): got_far = lax.all_to_all(far, 'dom', 0, 0, tiled=True)]
    pallas_call x3, Pallas kernels: 13.5 us -> 8.88 us  [the longest x1 3.67 us: body(): pl.pallas_call(main_kernel, out_shape=(pltpu.HBM(far_shape.shape, BF16),)...]
    ppermute x8, starting transfers between devices: 23.9 us -> 27.2 us  [exchange_near(): lax.ppermute(block, 'dom', [(a, (a + step) % N_DOM) for a in range(N_DOM)])]
  transfers between devices with their start and end apart: 10 -> 10, of which waited for: 5 -> 3; matrix products, arithmetic and copies ran while one was open for 1% -> 0% of each run, Pallas kernels for 3% -> 2%
where the time goes in v3:
time: 116 us; the launch traced here: 115 us
  starting transfers between devices  54.3 us (47%)
  waiting for transfers between devices  32.7 us (28%)
  blocking collectives  12.8 us (11%)
  Pallas kernels  11.7 us (10%)
  local copies, waits for them, and re-layouts  2.29 us (2%)
    ppermute x8, starting transfers between devices, exchange_near(): lax.ppermute(block, 'dom', [(a, (a + step) % N_DOM) for a in range(N_DOM)])  27.2 us
    all_to_all x1, waiting for transfers between devices, body(): back_far = lax.all_to_all(far_adj, 'dom', 0, 0, tiled=True)  23.5 us
    all_to_all x1, starting transfers between devices, body(): got_far = lax.all_to_all(far, 'dom', 0, 0, tiled=True)  19.3 us
    all_to_all x1, blocking collectives, body(): got = lax.all_to_all(outgoing, 'rep', 0, 0, tiled=True)  12.8 us
    all_to_all x1, waiting for transfers between devices, body(): got_far = lax.all_to_all(far, 'dom', 0, 0, tiled=True)  8.25 us
    all_to_all x1, starting transfers between devices, body(): back_far = lax.all_to_all(far_adj, 'dom', 0, 0, tiled=True)  7.86 us
    pallas_call x1, Pallas kernels, body(): pl.pallas_call(main_kernel, out_shape=(pltpu.HBM(far_shape.shape, BF16),)...  3.67 us
    pallas_call x1, Pallas kernels, body(): pl.pallas_call(pack_kernel, out_shape=(far_shape,) + (near_shape,) * BLOC...  3.14 us
  transfers between devices with their start and end apart: 10, of which 3 were waited for; matrix products, arithmetic and copies ran while one was open for 0% of the time, Pallas kernels for 2%

profile of v3, /device:TPU:32, one launch (start us, length us, event | category | flops | bytes accessed | tf_op | source)
XLA Modules:
  0.0 114.9 jit_solution(17369939537145182453)
XLA Ops:
  0.0 3.1 %pack.1 = (bf16[128,2,602]{2,1,0:T(2,128)(2,1)}, bf16[4,2,602]{2,1,0:T(2,128)(2,1)}, bf16[4,2,602]{2,1,0:T(2,128)(2,1)}, bf16[4,2,602]{2,1,0:T(2,128)(2,1)}, bf1...) custom-call(s32[1]{0:T(128)} %bitcast.dom_ref, s32[16,128]{1,0:T(8,128)} %bitcast.37, bf16[300,1024]{1,0:T(8,128)(2,1)} %prof_ref.1), custom_call_target="tpu_custom_call" | custom-call | tf_op jit(solution)/shard_map/pack/pallas_call | solution.py:171
  3.2 0.0 copy-start.3
  3.2 0.0 copy-start.5
  3.2 0.0 copy-start.6
  3.2 19.3 %all-to-all-start = ((bf16[128,2,602]{2,1,0:T(2,128)(2,1)}), bf16[128,2,602]{2,1,0:T(2,128)(2,1)S(1)}, u32[]{:S(2)}, u32[]{:S(2)}) async-start(bf16[128,2,602]{2,1,0:T(2,128)(2,1)} %get-tuple-element.21), calls=%async_computation | async-start | bytes 655360 | tf_op jit(solution)/shard_map/all_to_all | solution.py:192
  22.5 0.0 copy-start.1
  22.5 3.5 %collective-permute-start = (bf16[4,2,602]{2,1,0:T(2,128)(2,1)}, bf16[4,2,602]{2,1,0:T(2,128)(2,1)S(1)}, u32[]{:S(2)}, u32[]{:S(2)}) collective-permute-start(bf16[4,2,602]{2,1,0:T(2,128)(2,1)} %get-tuple-element.22), channel_id=1, source_target_pairs={{0,8},{4,12},{8,16},{12,20},{16,24},{20,28},{24,32},{28,36},{32,40... | collective-permute-start | bytes 28904 | tf_op jit(solution)/shard_map/ppermute | solution.py:157
  26.0 1.9 %collective-permute-start.1 = (bf16[4,2,602]{2,1,0:T(2,128)(2,1)}, bf16[4,2,602]{2,1,0:T(2,128)(2,1)S(1)}, u32[]{:S(2)}, u32[]{:S(2)}) collective-permute-start(bf16[4,2,602]{2,1,0:T(2,128)(2,1)} %get-tuple-element.23), channel_id=1, source_target_pairs={{0,4},{4,8},{8,12},{12,16},{16,20},{20,24},{24,28},{28,32},{32,36}... | collective-permute-start | bytes 28904 | tf_op jit(solution)/shard_map/ppermute | solution.py:157
  28.0 5.8 %collective-permute-start.2 = (bf16[4,2,602]{2,1,0:T(2,128)(2,1)}, bf16[4,2,602]{2,1,0:T(2,128)(2,1)S(1)}, u32[]{:S(2)}, u32[]{:S(2)}) collective-permute-start(bf16[4,2,602]{2,1,0:T(2,128)(2,1)} %get-tuple-element.25), channel_id=1, source_target_pairs={{0,508},{4,0},{8,4},{12,8},{16,12},{20,16},{24,20},{28,24},{32,28}... | collective-permute-start | bytes 28904 | tf_op jit(solution)/shard_map/ppermute | solution.py:157
  33.7 2.5 %collective-permute-start.3 = (bf16[4,2,602]{2,1,0:T(2,128)(2,1)S(1)}, bf16[4,2,602]{2,1,0:T(2,128)(2,1)S(1)}, u32[]{:S(2)}, u32[]{:S(2)}) collective-permute-start(bf16[4,2,602]{2,1,0:T(2,128)(2,1)S(1)} %copy-done.10), channel_id=1, source_target_pairs={{0,504},{4,508},{8,0},{12,4},{16,8},{20,12},{24,16},{28,20},{32,24... | collective-permute-start | bytes 28904 | tf_op jit(solution)/shard_map/ppermute | solution.py:157
  36.3 0.0 copy-start.8
  36.3 2.1 %prep.1 = (bf16[608,512]{1,0:T(8,128)(2,1)}, bf16[512,608]{1,0:T(8,128)(2,1)S(1)}, bf16[512,608]{1,0:T(8,128)(2,1)S(1)}, f32[512,512]{1,0:T(8,128)}) custom-call(s32[1]{0:T(128)} %bitcast.dom_ref, s32[4,512]{1,0:T(4,128)S(1)} %copy-done.5, f32[4,512]{1,0:T(4,128)S(1)} %copy-done.6, f32[100,512]{1,0:T(8,128)S(1)} %copy-done.2, bf16[100,512]{1,0:T(8,128)(2,1)S(1)} %bitcast.32), custom_call_target="tpu_custom_call" | custom-call | tf_op jit(solution)/shard_map/prep/pallas_call | solution.py:181
  38.3 0.0 collective-permute-done.refs_0_
  38.4 0.9 collective-permute-done.3.refs_4_
  39.3 8.3 %all-to-all-done.far_ref = bf16[128,2,602]{2,1,0:T(2,128)(2,1)S(1)} async-done(((bf16[128,2,602]{2,1,0:T(2,128)(2,1)}), bf16[128,2,602]{2,1,0:T(2,128)(2,1)S(1)}, u32[]{:S(2)}, u32[]{:S(2)}) %all-to-all-start) | async-done | bytes 308256 | tf_op jit(solution)/shard_map/all_to_all | solution.py:192
  47.6 0.7 copy-done.7
  48.2 3.7 %main.1 = (bf16[128,2,602]{2,1,0:T(2,128)(2,1)}, bf16[4,2,602]{2,1,0:T(2,128)(2,1)S(1)}, bf16[4,2,602]{2,1,0:T(2,128)(2,1)S(1)}, bf16[4,2,602]{2,1,0:T(2,128)(2,...) custom-call(bf16[128,2,602]{2,1,0:T(2,128)(2,1)S(1)} %all-to-all-done.far_ref, ...), custom_call_target="tpu_custom_call" | custom-call | tf_op jit(solution)/shard_map/main/pallas_call | solution.py:196
  51.9 2.5 %collective-permute-start.4 = (bf16[4,2,602]{2,1,0:T(2,128)(2,1)S(1)}, bf16[4,2,602]{2,1,0:T(2,128)(2,1)S(1)}, u32[]{:S(2)}, u32[]{:S(2)}) collective-permute-start(bf16[4,2,602]{2,1,0:T(2,128)(2,1)S(1)} %get-tuple-element.32), channel_id=1, source_target_pairs={{0,8},{4,12},{8,16},{12,20},{16,24},{20,28},{24,32},{28,36},{32,40... | collective-permute-start | bytes 28904 | tf_op jit(solution)/shard_map/ppermute | solution.py:157
  54.5 1.9 %collective-permute-start.5 = (bf16[4,2,602]{2,1,0:T(2,128)(2,1)S(1)}, bf16[4,2,602]{2,1,0:T(2,128)(2,1)S(1)}, u32[]{:S(2)}, u32[]{:S(2)}) collective-permute-start(bf16[4,2,602]{2,1,0:T(2,128)(2,1)S(1)} %get-tuple-element.33), channel_id=1, source_target_pairs={{0,4},{4,8},{8,12},{12,16},{16,20},{20,24},{24,28},{28,32},{32,36}... | collective-permute-start | bytes 28904 | tf_op jit(solution)/shard_map/ppermute | solution.py:157
  56.4 5.8 %collective-permute-start.6 = (bf16[4,2,602]{2,1,0:T(2,128)(2,1)S(1)}, bf16[4,2,602]{2,1,0:T(2,128)(2,1)S(1)}, u32[]{:S(2)}, u32[]{:S(2)}) collective-permute-start(bf16[4,2,602]{2,1,0:T(2,128)(2,1)S(1)} %get-tuple-element.35), channel_id=1, source_target_pairs={{0,508},{4,0},{8,4},{12,8},{16,12},{20,16},{24,20},{28,24},{32,28}... | collective-permute-start | bytes 28904 | tf_op jit(solution)/shard_map/ppermute | solution.py:157
  62.2 3.3 %collective-permute-start.7 = (bf16[4,2,602]{2,1,0:T(2,128)(2,1)S(1)}, bf16[4,2,602]{2,1,0:T(2,128)(2,1)S(1)}, u32[]{:S(2)}, u32[]{:S(2)}) collective-permute-start(bf16[4,2,602]{2,1,0:T(2,128)(2,1)S(1)} %get-tuple-element.36), channel_id=1, source_target_pairs={{0,504},{4,508},{8,0},{12,4},{16,8},{20,12},{24,16},{28,20},{32,24... | collective-permute-start | bytes 28904 | tf_op jit(solution)/shard_map/ppermute | solution.py:157
  65.5 7.9 %all-to-all-start.1 = ((bf16[128,2,602]{2,1,0:T(2,128)(2,1)}), bf16[128,2,602]{2,1,0:T(2,128)(2,1)S(1)}, u32[]{:S(2)}, u32[]{:S(2)}) async-start(bf16[128,2,602]{2,1,0:T(2,128)(2,1)} %get-tuple-element.31), calls=%async_computation.1 | async-start | bytes 655360 | tf_op jit(solution)/shard_map/all_to_all | solution.py:209
  73.5 0.0 copy-start.9
  73.5 0.6 copy-done.9
  74.1 0.0 slice-start
  74.2 0.6 slice-done
  74.8 0.1 broadcast_select_fusion
  74.9 23.5 %all-to-all-done.1 = bf16[128,2,602]{2,1,0:T(2,128)(2,1)S(1)} async-done(((bf16[128,2,602]{2,1,0:T(2,128)(2,1)}), bf16[128,2,602]{2,1,0:T(2,128)(2,1)S(1)}, u32[]{:S(2)}, u32[]{:S(2)}) %all-to-all-start.1) | async-done | bytes 308256 | tf_op jit(solution)/shard_map/all_to_all | solution.py:209
  98.4 0.2 copy.13
  98.6 0.6 pad_maximum_fusion
  99.2 12.8 %all_to_all.15.got_ref = bf16[4,38,2,602]{3,2,1,0:T(2,128)(2,1)} all-to-all(bf16[4,38,2,602]{3,2,1,0:T(2,128)(2,1)S(1)} %pad_maximum_fusion), channel_id=1, replica_groups=mesh['dom'=128,'rep'=4] {'rep'}, dimensions={0} | all-to-all | bytes 732032 | tf_op jit(solution)/shard_map/all_to_all | solution.py:217
  112.1 2.8 %final.1 = f32[300,256]{1,0:T(8,128)} custom-call(bf16[4,38,2,602]{3,2,1,0:T(2,128)(2,1)} %all_to_all.15.got_ref), custom_call_target="tpu_custom_call" | custom-call | tf_op jit(solution)/shard_map/final/pallas_call | solution.py:218
  (30 shorter events, 0.2 us)
Async XLA Ops:
  0.0 36.2 %copy-start.2 = (f32[100,512]{1,0:T(8,128)S(1)}, f32[100,512]{1,0:T(8,128)}, u32[]{:S(2)}) copy-start(f32[100,512]{1,0:T(8,128)} %dep_ref.1) | copy-start | bytes 614404
  3.1 44.4 %copy-start = (bf16[512,512]{1,0:T(8,128)(2,1)S(1)}, bf16[512,512]{1,0:T(8,128)(2,1)}, u32[]{:S(2)}) copy-start(bf16[512,512]{1,0:T(8,128)(2,1)} %refs_10_.1) | copy-start | bytes 1572868
  3.1 30.6 %copy-start.10 = (bf16[4,2,602]{2,1,0:T(2,128)(2,1)S(1)}, bf16[4,2,602]{2,1,0:T(2,128)(2,1)}, u32[]{:S(2)}) copy-start(bf16[4,2,602]{2,1,0:T(2,128)(2,1)} %get-tuple-element.26) | copy-start | bytes 28900
  3.2 33.1 %copy-start.3 = (bf16[512,100]{0,1:T(8,128)(2,1)S(1)}, bf16[512,100]{0,1:T(8,128)(2,1)}, u32[]{:S(2)}) copy-start(bf16[512,100]{0,1:T(8,128)(2,1)} %param.19) | copy-start | bytes 307204
  3.2 33.1 %copy-start.5 = (s32[4,512]{1,0:T(4,128)S(1)}, s32[4,512]{1,0:T(4,128)}, u32[]{:S(2)}) copy-start(s32[4,512]{1,0:T(4,128)} %slot_ref.1) | copy-start | bytes 24580
  3.2 33.1 %copy-start.6 = (f32[4,512]{1,0:T(4,128)S(1)}, f32[4,512]{1,0:T(4,128)}, u32[]{:S(2)}) copy-start(f32[4,512]{1,0:T(4,128)} %weight_ref.1) | copy-start | bytes 24580
  3.2 44.4 %all-to-all-start = ((bf16[128,2,602]{2,1,0:T(2,128)(2,1)}), bf16[128,2,602]{2,1,0:T(2,128)(2,1)S(1)}, u32[]{:S(2)}, u32[]{:S(2)}) async-start(bf16[128,2,602]{2,1,0:T(2,128)(2,1)} %get-tuple-element.21), calls=%async_computation | async-start | bytes 655360 | tf_op jit(solution)/shard_map/all_to_all | solution.py:192
  22.5 25.0 %copy-start.1 = (bf16[300,512]{1,0:T(8,128)(2,1)S(1)}, bf16[300,512]{1,0:T(8,128)(2,1)}, u32[]{:S(2)}) copy-start(bf16[300,512]{1,0:T(8,128)(2,1)} %refs_9_.1) | copy-start | bytes 921604
  22.5 15.8 %collective-permute-start = (bf16[4,2,602]{2,1,0:T(2,128)(2,1)}, bf16[4,2,602]{2,1,0:T(2,128)(2,1)S(1)}, u32[]{:S(2)}, u32[]{:S(2)}) collective-permute-start(bf16[4,2,602]{2,1,0:T(2,128)(2,1)} %get-tuple-element.22), channel_id=1, source_target_pairs={{0,8},{4,12},{8,16},{12,20},{16,24},{20,28},{24,32},{28,36},{32,40... | collective-permute-start | bytes 28904 | tf_op jit(solution)/shard_map/ppermute | solution.py:157
  26.0 12.3 %collective-permute-start.1 = (bf16[4,2,602]{2,1,0:T(2,128)(2,1)}, bf16[4,2,602]{2,1,0:T(2,128)(2,1)S(1)}, u32[]{:S(2)}, u32[]{:S(2)}) collective-permute-start(bf16[4,2,602]{2,1,0:T(2,128)(2,1)} %get-tuple-element.23), channel_id=1, source_target_pairs={{0,4},{4,8},{8,12},{12,16},{16,20},{20,24},{24,28},{28,32},{32,36}... | collective-permute-start | bytes 28904 | tf_op jit(solution)/shard_map/ppermute | solution.py:157
  28.0 10.4 %collective-permute-start.2 = (bf16[4,2,602]{2,1,0:T(2,128)(2,1)}, bf16[4,2,602]{2,1,0:T(2,128)(2,1)S(1)}, u32[]{:S(2)}, u32[]{:S(2)}) collective-permute-start(bf16[4,2,602]{2,1,0:T(2,128)(2,1)} %get-tuple-element.25), channel_id=1, source_target_pairs={{0,508},{4,0},{8,4},{12,8},{16,12},{20,16},{24,20},{28,24},{32,28}... | collective-permute-start | bytes 28904 | tf_op jit(solution)/shard_map/ppermute | solution.py:157
  33.7 5.6 %collective-permute-start.3 = (bf16[4,2,602]{2,1,0:T(2,128)(2,1)S(1)}, bf16[4,2,602]{2,1,0:T(2,128)(2,1)S(1)}, u32[]{:S(2)}, u32[]{:S(2)}) collective-permute-start(bf16[4,2,602]{2,1,0:T(2,128)(2,1)S(1)} %copy-done.10), channel_id=1, source_target_pairs={{0,504},{4,508},{8,0},{12,4},{16,8},{20,12},{24,16},{28,20},{32,24... | collective-permute-start | bytes 28904 | tf_op jit(solution)/shard_map/ppermute | solution.py:157
  36.3 11.3 %copy-start.8 = (f32[512]{0:T(512)S(1)}, f32[512]{0:T(512)}, u32[]{:S(2)}) copy-start(f32[512]{0:T(512)} %param.18) | copy-start | bytes 6148
  38.3 9.2 %copy-start.4 = (bf16[4,2,602]{2,1,0:T(2,128)(2,1)S(1)}, bf16[4,2,602]{2,1,0:T(2,128)(2,1)}, u32[]{:S(2)}) copy-start(bf16[4,2,602]{2,1,0:T(2,128)(2,1)} %get-tuple-element.24.refs_2_) | copy-start | bytes 28900
  47.6 0.7 copy-start.7
  51.9 21.5 %collective-permute-start.4 = (bf16[4,2,602]{2,1,0:T(2,128)(2,1)S(1)}, bf16[4,2,602]{2,1,0:T(2,128)(2,1)S(1)}, u32[]{:S(2)}, u32[]{:S(2)}) collective-permute-start(bf16[4,2,602]{2,1,0:T(2,128)(2,1)S(1)} %get-tuple-element.32), channel_id=1, source_target_pairs={{0,8},{4,12},{8,16},{12,20},{16,24},{20,28},{24,32},{28,36},{32,40... | collective-permute-start | bytes 28904 | tf_op jit(solution)/shard_map/ppermute | solution.py:157
  54.5 18.9 %collective-permute-start.5 = (bf16[4,2,602]{2,1,0:T(2,128)(2,1)S(1)}, bf16[4,2,602]{2,1,0:T(2,128)(2,1)S(1)}, u32[]{:S(2)}, u32[]{:S(2)}) collective-permute-start(bf16[4,2,602]{2,1,0:T(2,128)(2,1)S(1)} %get-tuple-element.33), channel_id=1, source_target_pairs={{0,4},{4,8},{8,12},{12,16},{16,20},{20,24},{24,28},{28,32},{32,36}... | collective-permute-start | bytes 28904 | tf_op jit(solution)/shard_map/ppermute | solution.py:157
  56.4 17.0 %collective-permute-start.6 = (bf16[4,2,602]{2,1,0:T(2,128)(2,1)S(1)}, bf16[4,2,602]{2,1,0:T(2,128)(2,1)S(1)}, u32[]{:S(2)}, u32[]{:S(2)}) collective-permute-start(bf16[4,2,602]{2,1,0:T(2,128)(2,1)S(1)} %get-tuple-element.35), channel_id=1, source_target_pairs={{0,508},{4,0},{8,4},{12,8},{16,12},{20,16},{24,20},{28,24},{32,28}... | collective-permute-start | bytes 28904 | tf_op jit(solution)/shard_map/ppermute | solution.py:157
  62.2 11.3 %collective-permute-start.7 = (bf16[4,2,602]{2,1,0:T(2,128)(2,1)S(1)}, bf16[4,2,602]{2,1,0:T(2,128)(2,1)S(1)}, u32[]{:S(2)}, u32[]{:S(2)}) collective-permute-start(bf16[4,2,602]{2,1,0:T(2,128)(2,1)S(1)} %get-tuple-element.36), channel_id=1, source_target_pairs={{0,504},{4,508},{8,0},{12,4},{16,8},{20,12},{24,16},{28,20},{32,24... | collective-permute-start | bytes 28904 | tf_op jit(solution)/shard_map/ppermute | solution.py:157
  65.5 32.9 %all-to-all-start.1 = ((bf16[128,2,602]{2,1,0:T(2,128)(2,1)}), bf16[128,2,602]{2,1,0:T(2,128)(2,1)S(1)}, u32[]{:S(2)}, u32[]{:S(2)}) async-start(bf16[128,2,602]{2,1,0:T(2,128)(2,1)} %get-tuple-element.31), calls=%async_computation.1 | async-start | bytes 655360 | tf_op jit(solution)/shard_map/all_to_all | solution.py:209
  73.5 0.6 copy-start.9
  74.1 0.7 slice-start

commit v4 on v3

v4 whole, which is shorter than its diff:
```python
import jax
import jax.numpy as jnp
from jax import lax
from jax.experimental import pallas as pl
from jax.experimental.pallas import tpu as pltpu
from jax.sharding import PartitionSpec as P


F32 = jnp.float32
BF16 = jnp.bfloat16
N_DOM = 128
N_REP = 4
CAP = 16
FAR = 4
REACH = 2
FEAT = 300
WIDE = FEAT + 1
PAIR = 2 * WIDE
FAR_ROWS = N_DOM * FAR // 2
NEAR_ROWS = (CAP - FAR) // 2
NEAR_STEP = 8
NEAR_PAD = 48
ROWS = FAR_ROWS + NEAR_PAD
QUARTER = 256
COLS = 1024
KERNEL_VMEM = 24 * 2**20


def dot(a, b, ca, cb):
    return lax.dot_general(a, b, (((ca,), (cb,)), ((), ())), preferred_element_type=F32)


def near_rows(rows, i):
    start = FAR_ROWS + i * NEAR_STEP
    return rows[start : start + NEAR_STEP].reshape(NEAR_STEP // 2, 2, PAIR)


def pack_kernel(dom_ref, lists_ref, prof_hbm, far_ref, home_ref, swap_ref, below_ref, above_ref, idx_ref, prof_ref, sem):
    load = pltpu.make_async_copy(prof_hbm, prof_ref, sem)
    load.start()
    idx = lists_ref[...].T
    idx_ref[...] = idx
    pairs = jnp.broadcast_to(idx[:, None, :], (N_DOM, FAR // 2, CAP)).reshape(FAR_ROWS, CAP)
    first = lax.broadcasted_iota(jnp.int32, (FAR_ROWS, 1), 0) % 2 == 0
    row = lax.broadcasted_iota(jnp.int32, (NEAR_PAD, CAP), 0)
    slot = lax.broadcasted_iota(jnp.int32, (NEAR_PAD, CAP), 1)
    around = jnp.zeros((NEAR_PAD, CAP), jnp.int32)
    dom = dom_ref[0]
    toward = 1 - 2 * (dom % 2)
    for i, step in enumerate((0, toward, -toward, -REACH, REACH)):
        other = idx_ref[pl.ds((dom + step + N_DOM) % N_DOM, 1), :]
        around = jnp.where(row // NEAR_STEP == i, other, around)
    around = around.astype(F32)
    lane = lax.broadcasted_iota(jnp.int32, (ROWS, COLS), 1)
    cols, picks = [], []
    for p in range(2):
        near_col = jnp.sum(
            jnp.where(slot == FAR + 2 * (row % NEAR_STEP) + p, around, 0.0), axis=1, keepdims=True
        ).astype(jnp.int32)
        far_col = jnp.where(first, pairs[:, p : p + 1], pairs[:, 2 + p : 3 + p])
        col = jnp.concatenate([far_col, near_col], axis=0)
        cols.append((col % QUARTER).astype(F32))
        picks.append(jnp.where(col == lane, 1.0, 0.0).astype(BF16))
    load.wait()
    prof = prof_ref[...]
    rows = jnp.concatenate(
        [dot(picks[0], prof, 1, 1), cols[0], dot(picks[1], prof, 1, 1), cols[1]], axis=1
    ).astype(BF16)
    far_ref[...] = rows[:FAR_ROWS].reshape(far_ref.shape)
    home_ref[...] = near_rows(rows, 0)
    half = NEAR_STEP // 2
    swap_ref[:half] = near_rows(rows, 1)
    swap_ref[half:] = near_rows(rows, 2)
    below_ref[...] = near_rows(rows, 3)
    above_ref[...] = near_rows(rows, 4)


def prep_kernel(
    dom_ref, slot_ref, weight_ref, dep_ref, w_out_ref,
    hi_ref, hi_t_ref, lo_t_ref, seed_ref,
):
    slot = slot_ref[...]
    owner = slot // CAP
    j = slot % CAP
    dom = dom_ref[0]
    odd = dom % 2
    apart = (owner - dom + REACH) % N_DOM
    block = jnp.where(apart == REACH, 0, jnp.where(apart == 2 * REACH, 2, 3))
    block = jnp.where(apart == REACH + 1, 1 + 3 * odd, block)
    block = jnp.where(apart == REACH - 1, 5 - 4 * odd, block)
    row = jnp.where(
        j < FAR, owner * (FAR // 2) + j // 2, FAR_ROWS + block * NEAR_STEP + (j - FAR) // 2
    )
    row = row + ROWS * (j % 2)
    index = lax.broadcasted_iota(jnp.int32, (2 * ROWS, slot.shape[1]), 0)
    acc = jnp.zeros(index.shape, F32)
    for k in range(4):
        acc = acc + jnp.where(row[k : k + 1] == index, weight_ref[k : k + 1], 0.0)
    hi = acc.astype(BF16)
    lo = acc - hi.astype(F32)
    hi_ref[...] = hi
    hi_t_ref[...] = acc.T.astype(BF16)
    lo_t_ref[...] = lo.T.astype(BF16)
    seed_ref[...] = dot(dep_ref[...].astype(BF16), w_out_ref[...], 0, 0)


def main_kernel(
    dom_ref, far_ref, home_ref, swap_ref, down_ref, up_ref,
    hi_t_ref, lo_t_ref, b_in_ref, b_mid_ref, w_in_ref, w_mid_ref, seed_hbm, hi_hbm,
    far_out_ref, home_out_ref, swap_out_ref, below_out_ref, above_out_ref,
    seed_ref, hi_ref, sems,
):
    remote, held = (seed_hbm, hi_hbm), (seed_ref, hi_ref)
    copies = [pltpu.make_async_copy(a, b, sems.at[i]) for i, (a, b) in enumerate(zip(remote, held))]
    for copy in copies:
        copy.start()

    def ready(i):
        copies[i].wait()
        return held[i][...]

    half = NEAR_STEP // 2
    near = (home_ref[...], swap_ref[:half], down_ref[:half], up_ref[:half], down_ref[half:], up_ref[half:])
    parts = [far_ref[...].reshape(FAR_ROWS, PAIR)]
    parts += [x.reshape(NEAR_STEP, PAIR) for x in near]
    fetched = jnp.concatenate(parts, axis=0)
    values = jnp.concatenate([fetched[:, :FEAT], fetched[:, WIDE : WIDE + FEAT]], axis=0)
    inputs = (dot(hi_t_ref[...], values, 1, 0) + dot(lo_t_ref[...], values, 1, 0)).astype(BF16)
    w_in = w_in_ref[...]
    t_one = jnp.tanh(dot(inputs, w_in, 1, 0) + b_in_ref[...])
    w_mid = w_mid_ref[...]
    t_two = jnp.tanh(dot(t_one.astype(BF16), w_mid, 1, 0) + b_mid_ref[...])
    g_two = (ready(0) * (1.0 - t_two * t_two)).astype(BF16)
    g_one = (dot(g_two, w_mid, 1, 1) * (1.0 - t_one * t_one)).astype(BF16)
    g_inputs = dot(g_one, w_in, 1, 1).astype(BF16)
    slots = dot(ready(1), g_inputs, 1, 0)
    rows = jnp.concatenate(
        [
            slots[:ROWS], fetched[:, FEAT:WIDE].astype(F32),
            slots[ROWS:], fetched[:, WIDE + FEAT :].astype(F32),
        ],
        axis=1,
    ).astype(BF16)
    far_out_ref[...] = rows[:FAR_ROWS].reshape(far_out_ref.shape)
    odd = dom_ref[0] % 2 == 1
    home_out_ref[...] = near_rows(rows, 0)
    swap_out_ref[:half] = near_rows(rows, 1)
    swap_out_ref[half:] = jnp.where(odd, near_rows(rows, 4), near_rows(rows, 5))
    below_out_ref[...] = near_rows(rows, 3)
    above_out_ref[...] = near_rows(rows, 2)


def final_kernel(got_ref, out_ref):
    got = got_ref[...].reshape(-1, PAIR)
    lane = lax.broadcasted_iota(jnp.int32, (got.shape[0], QUARTER), 1).astype(F32)
    total = None
    for p in range(2):
        place = got[:, p * WIDE + FEAT : (p + 1) * WIDE].astype(F32)
        pick = jnp.where(place == lane, 1.0, 0.0).astype(BF16)
        part = dot(got[:, p * WIDE : p * WIDE + FEAT], pick, 0, 0)
        total = part if total is None else total + part
    out_ref[...] = total


def shape(dims, dtype):
    return jax.ShapeDtypeStruct(dims, dtype)


def exchange_near(swap, below, above):
    half = NEAR_STEP // 2
    swapped = lax.ppermute(swap, "dom", [(a, a ^ 1) for a in range(N_DOM)])
    moved = [swapped]
    for block, step in ((below, -REACH), (above, REACH)):
        both = jnp.concatenate([block, swapped[half:]], axis=0)
        moved.append(lax.ppermute(both, "dom", [(a, (a + step) % N_DOM) for a in range(N_DOM)]))
    return moved


def body(
    profiles, pack_index, obs_slot, interp_weight, departures, w_in, b_in, w_mid, b_mid, w_out
):
    dom = lax.axis_index("dom")
    dom_scalar = dom.reshape(1).astype(jnp.int32)
    smem = pl.BlockSpec(memory_space=pltpu.SMEM)
    vmem = pl.BlockSpec(memory_space=pltpu.VMEM)
    far_dims = (N_DOM, FAR // 2, PAIR)
    one_dims, two_dims = (NEAR_STEP // 2, 2, PAIR), (NEAR_STEP, 2, PAIR)
    packed_shapes = tuple(pltpu.HBM(x, BF16) for x in (far_dims, one_dims, two_dims, one_dims, one_dims))
    hbm = pl.BlockSpec(memory_space=pltpu.HBM)
    far, home, swap, below, above = pl.pallas_call(
        pack_kernel,
        out_shape=packed_shapes,
        in_specs=[smem, vmem, hbm],
        scratch_shapes=[
            pltpu.VMEM((N_DOM, CAP), jnp.int32), pltpu.VMEM(profiles.shape, BF16), pltpu.SemaphoreType.DMA,
        ],
        name="pack",
    )(dom_scalar, pack_index[0, 0].T, profiles)

    obs = obs_slot.shape[1]
    hidden = w_mid.shape[0]
    hi, hi_t, lo_t, seed = pl.pallas_call(
        prep_kernel,
        out_shape=(
            pltpu.HBM((2 * ROWS, obs), BF16), pltpu.VMEM((obs, 2 * ROWS), BF16),
            pltpu.VMEM((obs, 2 * ROWS), BF16), pltpu.HBM((obs, hidden), F32),
        ),
        in_specs=[smem] + [vmem] * 4,
        compiler_params=pltpu.CompilerParams(vmem_limit_bytes=KERNEL_VMEM),
        name="prep",
    )(dom_scalar, obs_slot, interp_weight, departures, w_out.T)

    got_far = lax.all_to_all(far, "dom", 0, 0, tiled=True)
    got_near = exchange_near(swap, below, above)
    near_by = [pltpu.with_memory_space_constraint(x, pltpu.VMEM) for x in (got_far, hi_t, lo_t)]
    far_away = [pltpu.with_memory_space_constraint(x, pltpu.HBM) for x in (seed, hi)]
    far_adj, home_adj, swap_adj, below_adj, above_adj = pl.pallas_call(
        main_kernel,
        out_shape=packed_shapes,
        in_specs=[smem] + [vmem] * 11 + [hbm] * 2,
        scratch_shapes=[pltpu.VMEM(x.shape, x.dtype) for x in (seed, hi)]
        + [pltpu.SemaphoreType.DMA((2,))],
        compiler_params=pltpu.CompilerParams(vmem_limit_bytes=KERNEL_VMEM),
        name="main",
    )(
        dom_scalar, near_by[0], home, *got_near, near_by[1], near_by[2],
        b_in.reshape(1, -1), b_mid.reshape(1, -1), w_in, w_mid, *far_away,
    )

    back_far = lax.all_to_all(far_adj, "dom", 0, 0, tiled=True)
    swapped, down, up = exchange_near(swap_adj, below_adj, above_adj)
    half, kept = NEAR_STEP // 2, NEAR_ROWS // 2
    relayed = jnp.where(dom % 2 == 1, down[half : half + kept], up[half : half + kept])
    blocks = [home_adj[:kept], swapped[:kept], down[:kept], relayed]
    blocks = [jnp.where(dom % 2 == 1, blocks[i ^ 1], blocks[i]) for i in range(N_REP)]
    first = jnp.stack([jnp.where(dom % 4 >= 2, blocks[i ^ 2], blocks[i]) for i in range(N_REP)])
    owner = (jnp.arange(N_REP) == (dom + REACH) % N_REP).reshape(N_REP, 1, 1, 1)
    second = jnp.where(owner, up[:kept][None], jnp.zeros((), BF16))
    by_quarter = back_far.reshape(N_DOM // N_REP, N_REP, FAR // 2, PAIR).transpose(1, 0, 2, 3)
    outgoing = jnp.concatenate([by_quarter, first, second], axis=1)
    got = lax.all_to_all(outgoing, "rep", 0, 0, tiled=True)
    return pl.pallas_call(
        final_kernel, out_shape=shape((FEAT, QUARTER), F32), name="final"
    )(pltpu.with_memory_space_constraint(got, pltpu.VMEM))


def solution(mesh):
    placed = (
        P(None, "dom"),
        P("dom", "rep", None, None),
        P(None, ("dom", "rep")),
        P(None, ("dom", "rep")),
        P(None, ("dom", "rep")),
        P(),
        P(),
        P(),
        P(),
        P(),
    )
    return jax.shard_map(
        body, mesh=mesh, in_specs=placed, out_specs=P(None, ("dom", "rep")), check_vma=False
    )
```

time: 116 us -> 99.9 us (0.86)
  starting transfers between devices: 54.3 us -> 43 us
  waiting for transfers between devices: 32.7 us -> 29.6 us
  local copies, waits for them, and re-layouts: 2.29 us -> 0.97 us
    all_to_all x1, waiting for transfers between devices: 23.5 us -> 8.78 us  [body(): back_far = lax.all_to_all(far_adj, 'dom', 0, 0, tiled=True)]
    ppermute x8 -> x6, waiting for transfers between devices: 0.95 us -> 12.8 us  [the longest x4 10.6 us: exchange_near(): lax.ppermute(both, 'dom', [(a, (a + step) % N_DOM) for a in range(N_DOM)])]
    ppermute x8 -> x6, starting transfers between devices: 27.2 us -> 17.2 us  [the longest x4 13 us: exchange_near(): lax.ppermute(both, 'dom', [(a, (a + step) % N_DOM) for a in range(N_DOM)])]
    all_to_all x1, starting transfers between devices: 7.86 us -> 6.51 us  [body(): back_far = lax.all_to_all(far_adj, 'dom', 0, 0, tiled=True)]
  transfers between devices with their start and end apart: 10 -> 8, of which waited for: 3 -> 8; matrix products, arithmetic and copies ran while one was open for 0% -> 1% of each run, Pallas kernels for 2% -> 2%
where the time goes in v4:
time: 99.9 us; the launch traced here: 99.2 us
  starting transfers between devices  43 us (43%)
  waiting for transfers between devices  29.6 us (30%)
  blocking collectives  12.7 us (13%)
  Pallas kernels  11.1 us (11%)
  other arithmetic  1.57 us (2%)
    all_to_all x1, starting transfers between devices, body(): got_far = lax.all_to_all(far, 'dom', 0, 0, tiled=True)  19.3 us
    ppermute x4, starting transfers between devices, exchange_near(): lax.ppermute(both, 'dom', [(a, (a + step) % N_DOM) for a in range(N_DOM)])  13 us
    all_to_all x1, blocking collectives, body(): got = lax.all_to_all(outgoing, 'rep', 0, 0, tiled=True)  12.7 us
    ppermute x4, waiting for transfers between devices, exchange_near(): lax.ppermute(both, 'dom', [(a, (a + step) % N_DOM) for a in range(N_DOM)])  10.6 us
    all_to_all x1, waiting for transfers between devices, body(): back_far = lax.all_to_all(far_adj, 'dom', 0, 0, tiled=True)  8.78 us
    all_to_all x1, waiting for transfers between devices, body(): got_far = lax.all_to_all(far, 'dom', 0, 0, tiled=True)  8 us
    all_to_all x1, starting transfers between devices, body(): back_far = lax.all_to_all(far_adj, 'dom', 0, 0, tiled=True)  6.51 us
    ppermute x2, starting transfers between devices, exchange_near(): swapped = lax.ppermute(swap, 'dom', [(a, a ^ 1) for a in range(N_DOM)])  4.18 us
  transfers between devices with their start and end apart: 8, of which 8 were waited for; matrix products, arithmetic and copies ran while one was open for 1% of the time, Pallas kernels for 2%

profile of v4, /device:TPU:32, one launch (start us, length us, event | category | flops | bytes accessed | tf_op | source)
XLA Modules:
  0.0 99.2 jit_solution(16541756451426199253)
XLA Ops:
  0.0 3.5 %pack.1 = (bf16[128,2,602]{2,1,0:T(2,128)(2,1)}, bf16[4,2,602]{2,1,0:T(2,128)(2,1)}, bf16[8,2,602]{2,1,0:T(2,128)(2,1)}, bf16[4,2,602]{2,1,0:T(2,128)(2,1)}, bf16[4,2,602]{2,1,0:T(2,128)(2,1)}) custom-call(s32[1]{0:T(128)} %bitcast.dom_ref, s32[16,128]{1,0:T(8,128)} %bitcast.24, bf16[300,1024]{1,0:T(8,128)(2,1)} %prof_hbm.1), custom_call_target="tpu_custom_call" | custom-call | tf_op jit(solution)/shard_map/pack/pallas_call | solution.py:190
  3.5 0.0 copy-start.2
  3.5 0.0 copy-start.5
  3.5 0.0 copy-start.6
  3.5 0.0 copy-start
  3.5 19.3 %all-to-all-start = ((bf16[128,2,602]{2,1,0:T(2,128)(2,1)}), bf16[128,2,602]{2,1,0:T(2,128)(2,1)S(1)}, u32[]{:S(2)}, u32[]{:S(2)}) async-start(bf16[128,2,602]{2,1,0:T(2,128)(2,1)} %get-tuple-element.19), calls=%async_computation | async-start | bytes 655360 | tf_op jit(solution)/shard_map/all_to_all | solution.py:213
  22.8 0.0 copy-start.1
  22.9 2.2 %collective-permute-start = (bf16[8,2,602]{2,1,0:T(2,128)(2,1)}, bf16[8,2,602]{2,1,0:T(2,128)(2,1)S(1)}, u32[]{:S(2)}, u32[]{:S(2)}) collective-permute-start(bf16[8,2,602]{2,1,0:T(2,128)(2,1)} %get-tuple-element.21), channel_id=1, source_target_pairs={{0,4},{4,0},{8,12},{12,8},{16,20},{20,16},{24,28},{28,24},{32,36},... | collective-permute-start | bytes 57800 | tf_op jit(solution)/shard_map/ppermute | solution.py:171
  25.0 1.3 %collective-permute-done.swap_ref = bf16[8,2,602]{2,1,0:T(2,128)(2,1)S(1)} collective-permute-done((bf16[8,2,602]{2,1,0:T(2,128)(2,1)}, bf16[8,2,602]{2,1,0:T(2,128)(2,1)S(1)}, u32[]{:S(2)}, u32[]{:S(2)}) %collective-permute-start) | collective-permute-done | bytes 19296 | tf_op jit(solution)/shard_map/ppermute | solution.py:171
  26.3 0.8 pad_maximum_fusion.2
  27.1 4.6 %collective-permute-start.1 = (bf16[8,2,602]{2,1,0:T(2,128)(2,1)S(1)}, bf16[8,2,602]{2,1,0:T(2,128)(2,1)S(1)}, u32[]{:S(2)}, u32[]{:S(2)}) collective-permute-start(bf16[8,2,602]{2,1,0:T(2,128)(2,1)S(1)} %get-tuple-element.42), channel_id=1, source_target_pairs={{0,504},{4,508},{8,0},{12,4},{16,8},{20,12},{24,16},{28,20},{32,24... | collective-permute-start | bytes 57800 | tf_op jit(solution)/shard_map/ppermute | solution.py:175
  31.6 1.9 %collective-permute-start.2 = (bf16[8,2,602]{2,1,0:T(2,128)(2,1)S(1)}, bf16[8,2,602]{2,1,0:T(2,128)(2,1)S(1)}, u32[]{:S(2)}, u32[]{:S(2)}) collective-permute-start(bf16[8,2,602]{2,1,0:T(2,128)(2,1)S(1)} %get-tuple-element.41), channel_id=1, source_target_pairs={{0,8},{4,12},{8,16},{12,20},{16,24},{20,28},{24,32},{28,36},{32,40... | collective-permute-start | bytes 57800 | tf_op jit(solution)/shard_map/ppermute | solution.py:175
  33.6 0.0 copy-start.8
  33.6 2.1 %prep.1 = (bf16[608,512]{1,0:T(8,128)(2,1)}, bf16[512,608]{1,0:T(8,128)(2,1)S(1)}, bf16[512,608]{1,0:T(8,128)(2,1)S(1)}, f32[512,512]{1,0:T(8,128)}) custom-call(s32[1]{0:T(128)} %bitcast.dom_ref, s32[4,512]{1,0:T(4,128)S(1)} %copy-done.5, f32[4,512]{1,0:T(4,128)S(1)} %copy-done.6, f32[100,512]{1,0:T(8,128)S(1)} %copy-done.2, bf16[100,512]{1,0:T(8,128)(2,1)S(1)} %bitcast.19), custom_call_target="tpu_custom_call" | custom-call | tf_op jit(solution)/shard_map/prep/pallas_call | solution.py:202
  35.7 0.1 collective-permute-done.1.down_ref
  35.8 4.1 %collective-permute-done.2.up_ref = bf16[8,2,602]{2,1,0:T(2,128)(2,1)S(1)} collective-permute-done((bf16[8,2,602]{2,1,0:T(2,128)(2,1)S(1)}, bf16[8,2,602]{2,1,0:T(2,128)(2,1)S(1)}, u32[]{:S(2)}, u32[]{:S(2)}) %collective-permute-start.2) | collective-permute-done | bytes 19296 | tf_op jit(solution)/shard_map/ppermute | solution.py:175
  39.9 8.0 %all-to-all-done.far_ref = bf16[128,2,602]{2,1,0:T(2,128)(2,1)S(1)} async-done(((bf16[128,2,602]{2,1,0:T(2,128)(2,1)}), bf16[128,2,602]{2,1,0:T(2,128)(2,1)S(1)}, u32[]{:S(2)}, u32[]{:S(2)}) %all-to-all-start) | async-done | bytes 308256 | tf_op jit(solution)/shard_map/all_to_all | solution.py:213
  47.9 0.7 copy-done.7
  48.6 3.7 %main.1 = (bf16[128,2,602]{2,1,0:T(2,128)(2,1)}, bf16[4,2,602]{2,1,0:T(2,128)(2,1)}, bf16[8,2,602]{2,1,0:T(2,128)(2,1)}, bf16[4,2,602]{2,1,0:T(2,128)(2,1)}, bf16[4,2,602]{2,1,0:T(2,128)(2,1)}) custom-call(s32[1]{0:T(128)} %bitcast.dom_ref, bf16[128,2,602]{2,1,0:T(2,128)(2,1)S(1)} %all-to-all-done.far_ref, bf16[4,2,602]{2,1,0:T(2,128)(2,1)S(1)} %copy-done.4, ...), custom_call_target="tpu_custom_call" | custom-call | tf_op jit(solution)/shard_map/main/pallas_call | solution.py:217
  52.3 6.5 %all-to-all-start.1 = ((bf16[128,2,602]{2,1,0:T(2,128)(2,1)}), bf16[128,2,602]{2,1,0:T(2,128)(2,1)S(1)}, u32[]{:S(2)}, u32[]{:S(2)}) async-start(bf16[128,2,602]{2,1,0:T(2,128)(2,1)} %get-tuple-element.28), calls=%async_computation.1 | async-start | bytes 655360 | tf_op jit(solution)/shard_map/all_to_all | solution.py:230
  58.8 2.0 %collective-permute-start.3 = (bf16[8,2,602]{2,1,0:T(2,128)(2,1)S(1)}, bf16[8,2,602]{2,1,0:T(2,128)(2,1)S(1)}, u32[]{:S(2)}, u32[]{:S(2)}) collective-permute-start(bf16[8,2,602]{2,1,0:T(2,128)(2,1)S(1)} %copy-done.12), channel_id=1, source_target_pairs={{0,4},{4,0},{8,12},{12,8},{16,20},{20,16},{24,28},{28,24},{32,36},... | collective-permute-start | bytes 57800 | tf_op jit(solution)/shard_map/ppermute | solution.py:171
  60.9 1.0 %collective-permute-done.3 = bf16[8,2,602]{2,1,0:T(2,128)(2,1)S(1)} collective-permute-done((bf16[8,2,602]{2,1,0:T(2,128)(2,1)S(1)}, bf16[8,2,602]{2,1,0:T(2,128)(2,1)S(1)}, u32[]{:S(2)}, u32[]{:S(2)}) %collective-permute-start.3) | collective-permute-done | bytes 19296 | tf_op jit(solution)/shard_map/ppermute | solution.py:171
  62.0 4.6 %collective-permute-start.4 = (bf16[8,2,602]{2,1,0:T(2,128)(2,1)S(1)}, bf16[8,2,602]{2,1,0:T(2,128)(2,1)S(1)}, u32[]{:S(2)}, u32[]{:S(2)}) collective-permute-start(bf16[8,2,602]{2,1,0:T(2,128)(2,1)S(1)} %get-tuple-element.39), channel_id=1, source_target_pairs={{0,504},{4,508},{8,0},{12,4},{16,8},{20,12},{24,16},{28,20},{32,24... | collective-permute-start | bytes 57800 | tf_op jit(solution)/shard_map/ppermute | solution.py:175
  66.6 1.9 %collective-permute-start.5 = (bf16[8,2,602]{2,1,0:T(2,128)(2,1)S(1)}, bf16[8,2,602]{2,1,0:T(2,128)(2,1)S(1)}, u32[]{:S(2)}, u32[]{:S(2)}) collective-permute-start(bf16[8,2,602]{2,1,0:T(2,128)(2,1)S(1)} %get-tuple-element.40), channel_id=1, source_target_pairs={{0,8},{4,12},{8,16},{12,20},{16,24},{20,28},{24,32},{28,36},{32,40... | collective-permute-start | bytes 57800 | tf_op jit(solution)/shard_map/ppermute | solution.py:175
  68.5 3.2 %collective-permute-done.4 = bf16[8,2,602]{2,1,0:T(2,128)(2,1)S(1)} collective-permute-done((bf16[8,2,602]{2,1,0:T(2,128)(2,1)S(1)}, bf16[8,2,602]{2,1,0:T(2,128)(2,1)S(1)}, u32[]{:S(2)}, u32[]{:S(2)}) %collective-permute-start.4) | collective-permute-done | bytes 19296 | tf_op jit(solution)/shard_map/ppermute | solution.py:175
  71.8 3.1 %collective-permute-done.5 = bf16[8,2,602]{2,1,0:T(2,128)(2,1)S(1)} collective-permute-done((bf16[8,2,602]{2,1,0:T(2,128)(2,1)S(1)}, bf16[8,2,602]{2,1,0:T(2,128)(2,1)S(1)}, u32[]{:S(2)}, u32[]{:S(2)}) %collective-permute-start.5) | collective-permute-done | bytes 19296 | tf_op jit(solution)/shard_map/ppermute | solution.py:175
  74.9 0.1 broadcast_select_fusion
  75.1 8.8 %all-to-all-done.1 = bf16[128,2,602]{2,1,0:T(2,128)(2,1)S(1)} async-done(((bf16[128,2,602]{2,1,0:T(2,128)(2,1)}), bf16[128,2,602]{2,1,0:T(2,128)(2,1)S(1)}, u32[]{:S(2)}, u32[]{:S(2)}) %all-to-all-start.1) | async-done | bytes 308256 | tf_op jit(solution)/shard_map/all_to_all | solution.py:230
  83.8 0.2 copy.13
  84.1 0.6 pad_maximum_fusion
  84.7 12.7 %all_to_all.15.got_ref = bf16[4,38,2,602]{3,2,1,0:T(2,128)(2,1)S(1)} all-to-all(bf16[4,38,2,602]{3,2,1,0:T(2,128)(2,1)S(1)} %pad_maximum_fusion), channel_id=1, replica_groups=mesh['dom'=128,'rep'=4] {'rep'}, dimensions={0} | all-to-all | bytes 732032 | tf_op jit(solution)/shard_map/all_to_all | solution.py:241
  97.4 1.8 %final.1 = f32[300,256]{1,0:T(8,128)} custom-call(bf16[4,38,2,602]{3,2,1,0:T(2,128)(2,1)S(1)} %all_to_all.15.got_ref), custom_call_target="tpu_custom_call" | custom-call | tf_op jit(solution)/shard_map/final/pallas_call | solution.py:242
  (25 shorter events, 0.2 us)
Async XLA Ops:
  0.0 33.6 %copy-start.3 = (bf16[512,100]{0,1:T(8,128)(2,1)S(1)}, bf16[512,100]{0,1:T(8,128)(2,1)}, u32[]{:S(2)}) copy-start(bf16[512,100]{0,1:T(8,128)(2,1)} %param.19) | copy-start | bytes 307204
  3.5 30.1 %copy-start.2 = (f32[100,512]{1,0:T(8,128)S(1)}, f32[100,512]{1,0:T(8,128)}, u32[]{:S(2)}) copy-start(f32[100,512]{1,0:T(8,128)} %dep_ref.1) | copy-start | bytes 614404
  3.5 30.1 %copy-start.5 = (s32[4,512]{1,0:T(4,128)S(1)}, s32[4,512]{1,0:T(4,128)}, u32[]{:S(2)}) copy-start(s32[4,512]{1,0:T(4,128)} %slot_ref.1) | copy-start | bytes 24580
  3.5 30.1 %copy-start.6 = (f32[4,512]{1,0:T(4,128)S(1)}, f32[4,512]{1,0:T(4,128)}, u32[]{:S(2)}) copy-start(f32[4,512]{1,0:T(4,128)} %weight_ref.1) | copy-start | bytes 24580
  3.5 44.4 %copy-start = (bf16[512,512]{1,0:T(8,128)(2,1)S(1)}, bf16[512,512]{1,0:T(8,128)(2,1)}, u32[]{:S(2)}) copy-start(bf16[512,512]{1,0:T(8,128)(2,1)} %w_mid_ref.1) | copy-start | bytes 1572868
  3.5 44.4 %all-to-all-start = ((bf16[128,2,602]{2,1,0:T(2,128)(2,1)}), bf16[128,2,602]{2,1,0:T(2,128)(2,1)S(1)}, u32[]{:S(2)}, u32[]{:S(2)}) async-start(bf16[128,2,602]{2,1,0:T(2,128)(2,1)} %get-tuple-element.19), calls=%async_computation | async-start | bytes 655360 | tf_op jit(solution)/shard_map/all_to_all | solution.py:213
  22.8 25.1 %copy-start.1 = (bf16[300,512]{1,0:T(8,128)(2,1)S(1)}, bf16[300,512]{1,0:T(8,128)(2,1)}, u32[]{:S(2)}) copy-start(bf16[300,512]{1,0:T(8,128)(2,1)} %w_in_ref.1) | copy-start | bytes 921604
  22.9 3.4 %collective-permute-start = (bf16[8,2,602]{2,1,0:T(2,128)(2,1)}, bf16[8,2,602]{2,1,0:T(2,128)(2,1)S(1)}, u32[]{:S(2)}, u32[]{:S(2)}) collective-permute-start(bf16[8,2,602]{2,1,0:T(2,128)(2,1)} %get-tuple-element.21), channel_id=1, source_target_pairs={{0,4},{4,0},{8,12},{12,8},{16,20},{20,16},{24,28},{28,24},{32,36},... | collective-permute-start | bytes 57800 | tf_op jit(solution)/shard_map/ppermute | solution.py:171
  27.1 8.8 %collective-permute-start.1 = (bf16[8,2,602]{2,1,0:T(2,128)(2,1)S(1)}, bf16[8,2,602]{2,1,0:T(2,128)(2,1)S(1)}, u32[]{:S(2)}, u32[]{:S(2)}) collective-permute-start(bf16[8,2,602]{2,1,0:T(2,128)(2,1)S(1)} %get-tuple-element.42), channel_id=1, source_target_pairs={{0,504},{4,508},{8,0},{12,4},{16,8},{20,12},{24,16},{28,20},{32,24... | collective-permute-start | bytes 57800 | tf_op jit(solution)/shard_map/ppermute | solution.py:175
  31.6 8.2 %collective-permute-start.2 = (bf16[8,2,602]{2,1,0:T(2,128)(2,1)S(1)}, bf16[8,2,602]{2,1,0:T(2,128)(2,1)S(1)}, u32[]{:S(2)}, u32[]{:S(2)}) collective-permute-start(bf16[8,2,602]{2,1,0:T(2,128)(2,1)S(1)} %get-tuple-element.41), channel_id=1, source_target_pairs={{0,8},{4,12},{8,16},{12,20},{16,24},{20,28},{24,32},{28,36},{32,40... | collective-permute-start | bytes 57800 | tf_op jit(solution)/shard_map/ppermute | solution.py:175
  33.6 14.3 %copy-start.8 = (f32[512]{0:T(512)S(1)}, f32[512]{0:T(512)}, u32[]{:S(2)}) copy-start(f32[512]{0:T(512)} %param.18) | copy-start | bytes 6148
  35.7 12.2 %copy-start.4 = (bf16[4,2,602]{2,1,0:T(2,128)(2,1)S(1)}, bf16[4,2,602]{2,1,0:T(2,128)(2,1)}, u32[]{:S(2)}) copy-start(bf16[4,2,602]{2,1,0:T(2,128)(2,1)} %get-tuple-element.20.home_ref) | copy-start | bytes 28900
  47.9 0.7 copy-start.7
  52.3 6.5 %copy-start.12 = (bf16[8,2,602]{2,1,0:T(2,128)(2,1)S(1)}, bf16[8,2,602]{2,1,0:T(2,128)(2,1)}, u32[]{:S(2)}) copy-start(bf16[8,2,602]{2,1,0:T(2,128)(2,1)} %get-tuple-element.30) | copy-start | bytes 57796
  52.3 31.6 %all-to-all-start.1 = ((bf16[128,2,602]{2,1,0:T(2,128)(2,1)}), bf16[128,2,602]{2,1,0:T(2,128)(2,1)S(1)}, u32[]{:S(2)}, u32[]{:S(2)}) async-start(bf16[128,2,602]{2,1,0:T(2,128)(2,1)} %get-tuple-element.28), calls=%async_computation.1 | async-start | bytes 655360 | tf_op jit(solution)/shard_map/all_to_all | solution.py:230
  58.8 3.1 %collective-permute-start.3 = (bf16[8,2,602]{2,1,0:T(2,128)(2,1)S(1)}, bf16[8,2,602]{2,1,0:T(2,128)(2,1)S(1)}, u32[]{:S(2)}, u32[]{:S(2)}) collective-permute-start(bf16[8,2,602]{2,1,0:T(2,128)(2,1)S(1)} %copy-done.12), channel_id=1, source_target_pairs={{0,4},{4,0},{8,12},{12,8},{16,20},{20,16},{24,28},{28,24},{32,36},... | collective-permute-start | bytes 57800 | tf_op jit(solution)/shard_map/ppermute | solution.py:171
  60.8 1.1 %copy-start.10 = (bf16[4,2,602]{2,1,0:T(2,128)(2,1)S(1)}, bf16[4,2,602]{2,1,0:T(2,128)(2,1)}, u32[]{:S(2)}) copy-start(bf16[4,2,602]{2,1,0:T(2,128)(2,1)} %get-tuple-element.29) | copy-start | bytes 28900
  60.9 1.1 %copy-start.11 = (bf16[4,2,602]{2,1,0:T(2,128)(2,1)S(1)}, bf16[4,2,602]{2,1,0:T(2,128)(2,1)}, u32[]{:S(2)}) copy-start(bf16[4,2,602]{2,1,0:T(2,128)(2,1)} %get-tuple-element.31) | copy-start | bytes 28900
  62.0 9.8 %collective-permute-start.4 = (bf16[8,2,602]{2,1,0:T(2,128)(2,1)S(1)}, bf16[8,2,602]{2,1,0:T(2,128)(2,1)S(1)}, u32[]{:S(2)}, u32[]{:S(2)}) collective-permute-start(bf16[8,2,602]{2,1,0:T(2,128)(2,1)S(1)} %get-tuple-element.39), channel_id=1, source_target_pairs={{0,504},{4,508},{8,0},{12,4},{16,8},{20,12},{24,16},{28,20},{32,24... | collective-permute-start | bytes 57800 | tf_op jit(solution)/shard_map/ppermute | solution.py:175
  66.6 8.3 %collective-permute-start.5 = (bf16[8,2,602]{2,1,0:T(2,128)(2,1)S(1)}, bf16[8,2,602]{2,1,0:T(2,128)(2,1)S(1)}, u32[]{:S(2)}, u32[]{:S(2)}) collective-permute-start(bf16[8,2,602]{2,1,0:T(2,128)(2,1)S(1)} %get-tuple-element.40), channel_id=1, source_target_pairs={{0,8},{4,12},{8,16},{12,20},{16,24},{20,28},{24,32},{28,36},{32,40... | collective-permute-start | bytes 57800 | tf_op jit(solution)/shard_map/ppermute | solution.py:175
  68.5 6.4 %copy-start.9 = (bf16[4,2,602]{2,1,0:T(2,128)(2,1)S(1)}, bf16[4,2,602]{2,1,0:T(2,128)(2,1)}, u32[]{:S(2)}) copy-start(bf16[4,2,602]{2,1,0:T(2,128)(2,1)} %get-tuple-element.32) | copy-start | bytes 28900

commit v5 on v4

v5 whole, which is shorter than its diff:
```python
import jax
import jax.numpy as jnp
from jax import lax
from jax.experimental import pallas as pl
from jax.experimental.pallas import tpu as pltpu
from jax.sharding import Mesh, PartitionSpec as P


DOM = ("m", "q")
BY_QUARTER = ("q", "m")
F32 = jnp.float32
BF16 = jnp.bfloat16
N_DOM = 128
N_REP = 4
CAP = 16
FAR = 4
REACH = 2
FEAT = 300
WIDE = FEAT + 1
PAIR = 2 * WIDE
FAR_ROWS = N_DOM * FAR // 2
NEAR_ROWS = (CAP - FAR) // 2
NEAR_STEP = 8
NEAR_PAD = 48
ROWS = FAR_ROWS + NEAR_PAD
QUARTER = 256
QUARTER_ROWS = FAR_ROWS // N_REP
KERNEL_VMEM = 24 * 2**20


def dot(a, b, ca, cb):
    return lax.dot_general(a, b, (((ca,), (cb,)), ((), ())), preferred_element_type=F32)


def near_rows(rows, i):
    start = i * NEAR_STEP
    return rows[start : start + NEAR_STEP].reshape(NEAR_STEP // 2, 2, PAIR)


def pack_kernel(dom_ref, lists_ref, prof_hbm, far_ref, home_ref, swap_ref, below_ref, above_ref, idx_ref, prof_ref, sem):
    load = pltpu.make_async_copy(prof_hbm, prof_ref, sem)
    load.start()
    idx = lists_ref[...].T
    idx_ref[...] = idx
    row = lax.broadcasted_iota(jnp.int32, (NEAR_PAD, CAP), 0)
    slot = lax.broadcasted_iota(jnp.int32, (NEAR_PAD, CAP), 1)
    around = jnp.zeros((NEAR_PAD, CAP), jnp.int32)
    dom = dom_ref[0]
    toward = 1 - 2 * (dom % 2)
    for i, step in enumerate((0, toward, -toward, -REACH, REACH)):
        other = idx_ref[pl.ds((dom + step + N_DOM) % N_DOM, 1), :]
        around = jnp.where(row // NEAR_STEP == i, other, around)
    around = around.astype(F32)
    lane = lax.broadcasted_iota(jnp.int32, (1, QUARTER), 1).astype(F32).astype(BF16)
    one, zero = jnp.ones((), BF16), jnp.zeros((), BF16)
    near_col = jnp.concatenate(
        [
            jnp.sum(jnp.where(slot == FAR + 2 * (row % NEAR_STEP) + p, around, 0.0), axis=1, keepdims=True)
            for p in range(2)
        ],
        axis=0,
    ).astype(jnp.int32)
    near_place = (near_col % QUARTER).astype(F32)
    first = lax.broadcasted_iota(jnp.int32, (QUARTER_ROWS, 1), 0) % 2 == 0
    places, picks = [], []
    for q in range(N_REP):
        part = idx_ref[pl.ds(q, N_DOM // N_REP, stride=N_REP), :]
        part = jnp.broadcast_to(part[:, None, :], (N_DOM // N_REP, FAR // 2, CAP)).reshape(QUARTER_ROWS, CAP)
        col = jnp.concatenate(
            [jnp.where(first, part[:, p : p + 1], part[:, 2 + p : 3 + p]) for p in range(2)], axis=0
        )
        place = (col % QUARTER).astype(F32)
        here = jnp.where(near_col // QUARTER == q, near_place, -1.0)
        both = jnp.concatenate([place, here], axis=0).astype(BF16)
        places.append(place)
        picks.append(jnp.where(both == lane, one, zero))
    load.wait()
    near = None
    for q in range(N_REP):
        out = dot(picks[q], prof_ref[:, q * QUARTER : (q + 1) * QUARTER], 1, 1)
        n, place = QUARTER_ROWS, places[q]
        rows = jnp.concatenate([out[:n], place[:n], out[n : 2 * n], place[n:]], axis=1).astype(BF16)
        m = N_DOM // N_REP
        far_ref[q * m : (q + 1) * m] = rows.reshape(m, FAR // 2, PAIR)
        near = out[2 * n :] if near is None else near + out[2 * n :]
    n = NEAR_PAD
    rows = jnp.concatenate([near[:n], near_place[:n], near[n:], near_place[n:]], axis=1).astype(BF16)
    half = NEAR_STEP // 2
    home_ref[...] = near_rows(rows, 0)
    swap_ref[:half] = near_rows(rows, 1)
    swap_ref[half:] = near_rows(rows, 2)
    below_ref[...] = near_rows(rows, 3)
    above_ref[...] = near_rows(rows, 4)


def prep_kernel(
    dom_ref, slot_ref, weight_ref, dep_ref, w_out_ref, b_in_ref, b_mid_ref,
    hi_ref, both_t_ref, seed_ref, b_in_out_ref, b_mid_out_ref,
):
    slot = slot_ref[...]
    owner = slot // CAP
    j = slot % CAP
    dom = dom_ref[0]
    odd = dom % 2
    apart = (owner - dom + REACH) % N_DOM
    block = jnp.where(apart == REACH, 0, jnp.where(apart == 2 * REACH, 2, 3))
    block = jnp.where(apart == REACH + 1, 1 + 3 * odd, block)
    block = jnp.where(apart == REACH - 1, 5 - 4 * odd, block)
    place = owner % N_REP * (N_DOM // N_REP) + owner // N_REP
    row = jnp.where(
        j < FAR, place * (FAR // 2) + j // 2, FAR_ROWS + block * NEAR_STEP + (j - FAR) // 2
    )
    row = row + ROWS * (j % 2)
    index = lax.broadcasted_iota(jnp.int32, (2 * ROWS, slot.shape[1]), 0)
    acc = jnp.zeros(index.shape, F32)
    for k in range(4):
        acc = acc + jnp.where(row[k : k + 1] == index, weight_ref[k : k + 1], 0.0)
    hi = acc.astype(BF16)
    lo = acc - hi.astype(F32)
    hi_ref[...] = hi
    both_t_ref[...] = jnp.concatenate([acc.T, lo.T], axis=1).astype(BF16)
    b_in_out_ref[...] = b_in_ref[...]
    b_mid_out_ref[...] = b_mid_ref[...]
    seed_ref[...] = dot(dep_ref[...].astype(BF16), w_out_ref[...], 0, 0)


def main_kernel(
    dom_ref, far_ref, home_ref, swap_ref, down_ref, up_ref,
    both_t_ref, b_in_ref, b_mid_ref, w_in_ref, w_mid_ref, seed_hbm, hi_hbm,
    far_out_ref, home_out_ref, swap_out_ref, below_out_ref, above_out_ref,
    seed_ref, hi_ref, sems,
):
    remote, held = (seed_hbm, hi_hbm), (seed_ref, hi_ref)
    copies = [pltpu.make_async_copy(a, b, sems.at[i]) for i, (a, b) in enumerate(zip(remote, held))]
    for copy in copies:
        copy.start()

    def ready(i):
        copies[i].wait()
        return held[i][...]

    half = NEAR_STEP // 2
    near = (home_ref[...], swap_ref[:half], down_ref[:half], up_ref[:half], down_ref[half:], up_ref[half:])
    parts = [far_ref[...].reshape(FAR_ROWS, PAIR)]
    parts += [x.reshape(NEAR_STEP, PAIR) for x in near]
    fetched = jnp.concatenate(parts, axis=0)
    values = [fetched[:, :FEAT], fetched[:, WIDE : WIDE + FEAT]] * 2
    inputs = dot(both_t_ref[...], jnp.concatenate(values, axis=0), 1, 0).astype(BF16)
    w_in = w_in_ref[...]
    t_one = jnp.tanh(dot(inputs, w_in, 1, 0) + b_in_ref[...])
    w_mid = w_mid_ref[...]
    t_two = jnp.tanh(dot(t_one.astype(BF16), w_mid, 1, 0) + b_mid_ref[...])
    g_two = (ready(0) * (1.0 - t_two * t_two)).astype(BF16)
    g_one = (dot(g_two, w_mid, 1, 1) * (1.0 - t_one * t_one)).astype(BF16)
    g_inputs = dot(g_one, w_in, 1, 1).astype(BF16)
    slots = dot(ready(1), g_inputs, 1, 0)
    rows = jnp.concatenate(
        [
            slots[:ROWS], fetched[:, FEAT:WIDE].astype(F32),
            slots[ROWS:], fetched[:, WIDE + FEAT :].astype(F32),
        ],
        axis=1,
    ).astype(BF16)
    far_out_ref[...] = rows[:FAR_ROWS].reshape(far_out_ref.shape)
    rows = rows[FAR_ROWS:]
    odd = dom_ref[0] % 2 == 1
    home_out_ref[...] = near_rows(rows, 0)
    swap_out_ref[:half] = near_rows(rows, 1)
    swap_out_ref[half:] = jnp.where(odd, near_rows(rows, 4), near_rows(rows, 5))
    below_out_ref[...] = near_rows(rows, 3)
    above_out_ref[...] = near_rows(rows, 2)


def final_kernel(got_ref, out_ref):
    got = got_ref[...].reshape(-1, PAIR)
    lane = lax.broadcasted_iota(jnp.int32, (1, QUARTER), 1).astype(F32).astype(BF16)
    one, zero = jnp.ones((), BF16), jnp.zeros((), BF16)
    total = None
    for p in range(2):
        place = got[:, p * WIDE + FEAT : (p + 1) * WIDE]
        pick = jnp.where(place == lane, one, zero)
        part = dot(got[:, p * WIDE : p * WIDE + FEAT], pick, 0, 0)
        total = part if total is None else total + part
    out_ref[...] = total


def shape(dims, dtype):
    return jax.ShapeDtypeStruct(dims, dtype)


def exchange_near(swap, below, above):
    half = NEAR_STEP // 2
    swapped = lax.ppermute(swap, DOM, [(a, a ^ 1) for a in range(N_DOM)])
    moved = [swapped]
    for block, step in ((below, -REACH), (above, REACH)):
        both = jnp.concatenate([block, swapped[half:]], axis=0)
        moved.append(lax.ppermute(both, DOM, [(a, (a + step) % N_DOM) for a in range(N_DOM)]))
    return moved


def body(
    profiles, pack_index, obs_slot, interp_weight, departures, w_in, b_in, w_mid, b_mid, w_out
):
    dom = lax.axis_index(DOM)
    dom_scalar = dom.reshape(1).astype(jnp.int32)
    smem = pl.BlockSpec(memory_space=pltpu.SMEM)
    vmem = pl.BlockSpec(memory_space=pltpu.VMEM)
    far_dims = (N_DOM, FAR // 2, PAIR)
    one_dims, two_dims = (NEAR_STEP // 2, 2, PAIR), (NEAR_STEP, 2, PAIR)
    packed_shapes = (
        pltpu.HBM(far_dims, BF16), pltpu.VMEM(one_dims, BF16), pltpu.HBM(two_dims, BF16),
        pltpu.HBM(one_dims, BF16), pltpu.HBM(one_dims, BF16),
    )
    hbm = pl.BlockSpec(memory_space=pltpu.HBM)
    far, home, swap, below, above = pl.pallas_call(
        pack_kernel,
        out_shape=packed_shapes,
        in_specs=[smem, vmem, hbm],
        scratch_shapes=[
            pltpu.VMEM((N_DOM, CAP), jnp.int32), pltpu.VMEM(profiles.shape, BF16), pltpu.SemaphoreType.DMA,
        ],
        name="pack",
    )(dom_scalar, pack_index[0, 0].T, profiles)

    obs = obs_slot.shape[1]
    hidden = w_mid.shape[0]
    hi, both_t, seed, bias_in, bias_mid = pl.pallas_call(
        prep_kernel,
        out_shape=(
            pltpu.HBM((2 * ROWS, obs), BF16), pltpu.VMEM((obs, 4 * ROWS), BF16),
            pltpu.HBM((obs, hidden), F32),
            pltpu.VMEM((1, hidden), F32), pltpu.VMEM((1, hidden), F32),
        ),
        in_specs=[smem] + [vmem] * 6,
        compiler_params=pltpu.CompilerParams(vmem_limit_bytes=KERNEL_VMEM),
        name="prep",
    )(
        dom_scalar, obs_slot, interp_weight, departures, w_out.T,
        b_in.reshape(1, -1), b_mid.reshape(1, -1),
    )

    got_far = lax.all_to_all(far, BY_QUARTER, 0, 0, tiled=True)
    got_near = exchange_near(swap, below, above)
    near_by = [
        pltpu.with_memory_space_constraint(x, pltpu.VMEM)
        for x in (got_far, home, both_t, bias_in, bias_mid)
    ]
    far_away = [pltpu.with_memory_space_constraint(x, pltpu.HBM) for x in (seed, hi)]
    far_adj, home_adj, swap_adj, below_adj, above_adj = pl.pallas_call(
        main_kernel,
        out_shape=packed_shapes,
        in_specs=[smem] + [vmem] * 10 + [hbm] * 2,
        scratch_shapes=[pltpu.VMEM(x.shape, x.dtype) for x in (seed, hi)]
        + [pltpu.SemaphoreType.DMA((2,))],
        compiler_params=pltpu.CompilerParams(vmem_limit_bytes=KERNEL_VMEM),
        name="main",
    )(
        dom_scalar, *near_by[:2], *got_near, *near_by[2:], w_in, w_mid, *far_away,
    )

    back_far = lax.all_to_all(far_adj, BY_QUARTER, 0, 0, tiled=True)
    swapped, down, up = exchange_near(swap_adj, below_adj, above_adj)
    half, kept = NEAR_STEP // 2, NEAR_ROWS // 2
    relayed = jnp.where(dom % 2 == 1, down[half : half + kept], up[half : half + kept])
    blocks = [home_adj[:kept], swapped[:kept], down[:kept], relayed]
    blocks = [jnp.where(dom % 2 == 1, blocks[i ^ 1], blocks[i]) for i in range(N_REP)]
    first = jnp.stack([jnp.where(dom % 4 >= 2, blocks[i ^ 2], blocks[i]) for i in range(N_REP)])
    owner = (jnp.arange(N_REP) == (dom + REACH) % N_REP).reshape(N_REP, 1, 1, 1)
    second = jnp.where(owner, up[:kept][None], jnp.zeros((), BF16))
    by_quarter = back_far.reshape(N_REP, N_DOM // N_REP, FAR // 2, PAIR)
    outgoing = jnp.concatenate([by_quarter, first, second], axis=1)
    got = lax.all_to_all(outgoing, "rep", 0, 0, tiled=True)
    return pl.pallas_call(
        final_kernel, out_shape=shape((FEAT, QUARTER), F32), name="final"
    )(pltpu.with_memory_space_constraint(got, pltpu.VMEM))


def solution(mesh):
    cut = Mesh(mesh.devices.reshape(N_DOM // N_REP, N_REP, N_REP), DOM + ("rep",))
    all_axes = DOM + ("rep",)
    placed = (
        P(None, DOM),
        P(DOM, "rep", None, None),
        P(None, all_axes),
        P(None, all_axes),
        P(None, all_axes),
        P(),
        P(),
        P(),
        P(),
        P(),
    )
    return jax.shard_map(body, mesh=cut, in_specs=placed, out_specs=P(None, all_axes), check_vma=False)
```

time: 99.9 us -> 101 us (1.011)
  the two profiles are of different devices: /device:TPU:32 before, /device:TPU:1 now
where the time goes in v5:
time: 101 us; the launch traced here: 100 us
  starting transfers between devices  49.6 us (49%)
  waiting for transfers between devices  24.6 us (24%)
  blocking collectives  12.3 us (12%)
  Pallas kernels  10.9 us (11%)
  other arithmetic  2.29 us (2%)
    all_to_all x1, starting transfers between devices, body(): got_far = lax.all_to_all(far, BY_QUARTER, 0, 0, tiled=True)  20.7 us
    ppermute x4, starting transfers between devices, exchange_near(): lax.ppermute(both, DOM, [(a, (a + step) % N_DOM) for a in range(N_DOM)])  17.4 us
    all_to_all x1, blocking collectives, body(): got = lax.all_to_all(outgoing, 'rep', 0, 0, tiled=True)  12.3 us
    ppermute x4, waiting for transfers between devices, exchange_near(): lax.ppermute(both, DOM, [(a, (a + step) % N_DOM) for a in range(N_DOM)])  10.6 us
    all_to_all x1, starting transfers between devices, body(): back_far = lax.all_to_all(far_adj, BY_QUARTER, 0, 0, tiled=True)  6.17 us
    all_to_all x1, waiting for transfers between devices, body(): got_far = lax.all_to_all(far, BY_QUARTER, 0, 0, tiled=True)  6.08 us
    all_to_all x1, waiting for transfers between devices, body(): back_far = lax.all_to_all(far_adj, BY_QUARTER, 0, 0, tiled=True)  5.91 us
    ppermute x2, starting transfers between devices, exchange_near(): swapped = lax.ppermute(swap, DOM, [(a, a ^ 1) for a in range(N_DOM)])  5.4 us
  transfers between devices with their start and end apart: 8, of which 6 were waited for; matrix products, arithmetic and copies ran while one was open for 2% of the time, Pallas kernels for 2%

profile of v5, /device:TPU:1, one launch (start us, length us, event | category | flops | bytes accessed | tf_op | source)
XLA Modules:
  0.0 100.0 jit_solution(15964701733960724045)
XLA Ops:
  0.0 0.0 copy-start.4
  0.0 0.0 copy-start.5
  0.0 0.0 copy-start.2
  0.0 0.0 copy-start.1
  0.0 0.0 copy-start
  0.1 3.5 %pack.1 = (bf16[128,2,602]{2,1,0:T(2,128)(2,1)}, bf16[4,2,602]{2,1,0:T(2,128)(2,1)S(1)}, bf16[8,2,602]{2,1,0:T(2,128)(2,1)}, bf16[4,2,602]{2,1,0:T(2,128)(2,1)}, bf16[4,2,602]{2,1,0:T(2,128)(2,1)}) custom-call(s32[1]{0:T(128)} %bitcast.dom_ref, s32[16,128]{1,0:T(8,128)} %bitcast.20, bf16[300,1024]{1,0:T(8,128)(2,1)} %prof_hbm.1), custom_call_target="tpu_custom_call" | custom-call | tf_op jit(solution)/shard_map/pack/pallas_call | solution.py:215
  3.5 20.7 %all-to-all-start = ((bf16[128,2,602]{2,1,0:T(2,128)(2,1)}), bf16[128,2,602]{2,1,0:T(2,128)(2,1)S(1)}, u32[]{:S(2)}, u32[]{:S(2)}) async-start(bf16[128,2,602]{2,1,0:T(2,128)(2,1)} %get-tuple-element.20), calls=%async_computation | async-start | bytes 655360 | tf_op jit(solution)/shard_map/all_to_all | solution.py:242
  24.2 2.7 %collective-permute-start = (bf16[8,2,602]{2,1,0:T(2,128)(2,1)}, bf16[8,2,602]{2,1,0:T(2,128)(2,1)S(1)}, u32[]{:S(2)}, u32[]{:S(2)}) collective-permute-start(bf16[8,2,602]{2,1,0:T(2,128)(2,1)} %get-tuple-element.22), channel_id=1, source_target_pairs={{0,4},{4,0},{8,12},{12,8},{16,20},{20,16},{24,28},{28,24},{32,36},... | collective-permute-start | bytes 57800 | tf_op jit(solution)/shard_map/ppermute | solution.py:193
  26.9 1.0 %collective-permute-done.swap_ref = bf16[8,2,602]{2,1,0:T(2,128)(2,1)S(1)} collective-permute-done((bf16[8,2,602]{2,1,0:T(2,128)(2,1)}, bf16[8,2,602]{2,1,0:T(2,128)(2,1)S(1)}, u32[]{:S(2)}, u32[]{:S(2)}) %collective-permute-start) | collective-permute-done | bytes 19296 | tf_op jit(solution)/shard_map/ppermute | solution.py:193
  28.0 0.8 pad_maximum_fusion.2
  28.7 6.8 %collective-permute-start.1 = (bf16[8,2,602]{2,1,0:T(2,128)(2,1)S(1)}, bf16[8,2,602]{2,1,0:T(2,128)(2,1)S(1)}, u32[]{:S(2)}, u32[]{:S(2)}) collective-permute-start(bf16[8,2,602]{2,1,0:T(2,128)(2,1)S(1)} %get-tuple-element.44), channel_id=1, source_target_pairs={{0,504},{4,508},{8,0},{12,4},{16,8},{20,12},{24,16},{28,20},{32,24... | collective-permute-start | bytes 57800 | tf_op jit(solution)/shard_map/ppermute | solution.py:197
  35.5 1.9 %collective-permute-start.2 = (bf16[8,2,602]{2,1,0:T(2,128)(2,1)S(1)}, bf16[8,2,602]{2,1,0:T(2,128)(2,1)S(1)}, u32[]{:S(2)}, u32[]{:S(2)}) collective-permute-start(bf16[8,2,602]{2,1,0:T(2,128)(2,1)S(1)} %get-tuple-element.43), channel_id=1, source_target_pairs={{0,8},{4,12},{8,16},{12,20},{16,24},{20,28},{24,32},{28,36},{32,40... | collective-permute-start | bytes 57800 | tf_op jit(solution)/shard_map/ppermute | solution.py:197
  37.5 0.0 copy-done.3
  37.5 2.2 %prep.1 = (bf16[608,512]{1,0:T(8,128)(2,1)}, bf16[512,1216]{1,0:T(8,128)(2,1)S(1)}, f32[512,512]{1,0:T(8,128)}, f32[1,512]{1,0:T(1,128)S(1)}, f32[1,512]{1,0:T(1,128)S(1)}) custom-call(s32[1]{0:T(128)} %bitcast.dom_ref, s32[4,512]{1,0:T(4,128)S(1)} %copy-done.4, f32[4,512]{1,0:T(4,128)S(1)} %copy-done.5, f32[100,512]{1,0:T(8,128)S(1)} %copy-done.2, ...), custom_call_target="tpu_custom_call" | custom-call | tf_op jit(solution)/shard_map/prep/pallas_call | solution.py:227
  39.7 0.0 collective-permute-done.1.down_ref
  39.7 4.2 %collective-permute-done.2.up_ref = bf16[8,2,602]{2,1,0:T(2,128)(2,1)S(1)} collective-permute-done((bf16[8,2,602]{2,1,0:T(2,128)(2,1)S(1)}, bf16[8,2,602]{2,1,0:T(2,128)(2,1)S(1)}, u32[]{:S(2)}, u32[]{:S(2)}) %collective-permute-start.2) | collective-permute-done | bytes 19296 | tf_op jit(solution)/shard_map/ppermute | solution.py:197
  43.9 6.1 %all-to-all-done.far_ref = bf16[128,2,602]{2,1,0:T(2,128)(2,1)S(1)} async-done(((bf16[128,2,602]{2,1,0:T(2,128)(2,1)}), bf16[128,2,602]{2,1,0:T(2,128)(2,1)S(1)}, u32[]{:S(2)}, u32[]{:S(2)}) %all-to-all-start) | async-done | bytes 308256 | tf_op jit(solution)/shard_map/all_to_all | solution.py:242
  50.0 0.0 copy-done.1
  50.0 3.6 %main.1 = (bf16[128,2,602]{2,1,0:T(2,128)(2,1)}, bf16[4,2,602]{2,1,0:T(2,128)(2,1)S(1)}, bf16[8,2,602]{2,1,0:T(2,128)(2,1)}, bf16[4,2,602]{2,1,0:T(2,128)(2,1)}, bf16[4,2,602]{2,1,0:T(2,128)(2,1)}) custom-call(s32[1]{0:T(128)} %bitcast.dom_ref, bf16[128,2,602]{2,1,0:T(2,128)(2,1)S(1)} %all-to-all-done.far_ref, ...), custom_call_target="tpu_custom_call" | custom-call | tf_op jit(solution)/shard_map/main/pallas_call | solution.py:249
  53.5 6.2 %all-to-all-start.1 = ((bf16[128,2,602]{2,1,0:T(2,128)(2,1)}), bf16[128,2,602]{2,1,0:T(2,128)(2,1)S(1)}, u32[]{:S(2)}, u32[]{:S(2)}) async-start(bf16[128,2,602]{2,1,0:T(2,128)(2,1)} %get-tuple-element.30), calls=%async_computation.1 | async-start | bytes 655360 | tf_op jit(solution)/shard_map/all_to_all | solution.py:261
  59.7 2.7 %collective-permute-start.3 = (bf16[8,2,602]{2,1,0:T(2,128)(2,1)}, bf16[8,2,602]{2,1,0:T(2,128)(2,1)S(1)}, u32[]{:S(2)}, u32[]{:S(2)}) collective-permute-start(bf16[8,2,602]{2,1,0:T(2,128)(2,1)} %get-tuple-element.32), channel_id=1, source_target_pairs={{0,4},{4,0},{8,12},{12,8},{16,20},{20,16},{24,28},{28,24},{32,36},... | collective-permute-start | bytes 57800 | tf_op jit(solution)/shard_map/ppermute | solution.py:193
  62.4 1.0 %collective-permute-done.3 = bf16[8,2,602]{2,1,0:T(2,128)(2,1)S(1)} collective-permute-done((bf16[8,2,602]{2,1,0:T(2,128)(2,1)}, bf16[8,2,602]{2,1,0:T(2,128)(2,1)S(1)}, u32[]{:S(2)}, u32[]{:S(2)}) %collective-permute-start.3) | collective-permute-done | bytes 19296 | tf_op jit(solution)/shard_map/ppermute | solution.py:193
  63.5 0.8 pad_maximum_fusion.3
  64.2 6.8 %collective-permute-start.4 = (bf16[8,2,602]{2,1,0:T(2,128)(2,1)S(1)}, bf16[8,2,602]{2,1,0:T(2,128)(2,1)S(1)}, u32[]{:S(2)}, u32[]{:S(2)}) collective-permute-start(bf16[8,2,602]{2,1,0:T(2,128)(2,1)S(1)} %get-tuple-element.41), channel_id=1, source_target_pairs={{0,504},{4,508},{8,0},{12,4},{16,8},{20,12},{24,16},{28,20},{32,24... | collective-permute-start | bytes 57800 | tf_op jit(solution)/shard_map/ppermute | solution.py:197
  71.0 1.9 %collective-permute-start.5 = (bf16[8,2,602]{2,1,0:T(2,128)(2,1)S(1)}, bf16[8,2,602]{2,1,0:T(2,128)(2,1)S(1)}, u32[]{:S(2)}, u32[]{:S(2)}) collective-permute-start(bf16[8,2,602]{2,1,0:T(2,128)(2,1)S(1)} %get-tuple-element.42), channel_id=1, source_target_pairs={{0,8},{4,12},{8,16},{12,20},{16,24},{20,28},{24,32},{28,36},{32,40... | collective-permute-start | bytes 57800 | tf_op jit(solution)/shard_map/ppermute | solution.py:197
  73.0 0.0 collective-permute-done.4
  73.0 6.4 %collective-permute-done.5 = bf16[8,2,602]{2,1,0:T(2,128)(2,1)S(1)} collective-permute-done((bf16[8,2,602]{2,1,0:T(2,128)(2,1)S(1)}, bf16[8,2,602]{2,1,0:T(2,128)(2,1)S(1)}, u32[]{:S(2)}, u32[]{:S(2)}) %collective-permute-start.5) | collective-permute-done | bytes 19296 | tf_op jit(solution)/shard_map/ppermute | solution.py:197
  79.4 0.1 broadcast_select_fusion
  79.6 5.9 %all-to-all-done.1 = bf16[128,2,602]{2,1,0:T(2,128)(2,1)S(1)} async-done(((bf16[128,2,602]{2,1,0:T(2,128)(2,1)}), bf16[128,2,602]{2,1,0:T(2,128)(2,1)S(1)}, u32[]{:S(2)}, u32[]{:S(2)}) %all-to-all-start.1) | async-done | bytes 308256 | tf_op jit(solution)/shard_map/all_to_all | solution.py:261
  85.5 0.6 pad_maximum_fusion
  86.1 12.3 %all_to_all.15.got_ref = bf16[4,38,2,602]{3,2,1,0:T(2,128)(2,1)S(1)} all-to-all(bf16[4,38,2,602]{3,2,1,0:T(2,128)(2,1)S(1)} %pad_maximum_fusion), channel_id=1, replica_groups=mesh['m'=32,'q'=4,'rep'=4] {'rep'}, dimensions={0} | all-to-all | bytes 732032 | tf_op jit(solution)/shard_map/all_to_all | solution.py:272
  98.4 1.7 %final.1 = f32[300,256]{1,0:T(8,128)} custom-call(bf16[4,38,2,602]{3,2,1,0:T(2,128)(2,1)S(1)} %all_to_all.15.got_ref), custom_call_target="tpu_custom_call" | custom-call | tf_op jit(solution)/shard_map/final/pallas_call | solution.py:273
  (14 shorter events, 0.1 us)
Async XLA Ops:
  0.0 37.5 %copy-start.3 = (bf16[512,100]{0,1:T(8,128)(2,1)S(1)}, bf16[512,100]{0,1:T(8,128)(2,1)}, u32[]{:S(2)}) copy-start(bf16[512,100]{0,1:T(8,128)(2,1)} %param.19) | copy-start | bytes 307204
  0.0 37.5 %copy-start.6 = (f32[512]{0:T(512)S(1)}, f32[512]{0:T(512)}, u32[]{:S(2)}) copy-start(f32[512]{0:T(512)} %param.16) | copy-start | bytes 6148
  0.0 37.5 %copy-start.7 = (f32[512]{0:T(512)S(1)}, f32[512]{0:T(512)}, u32[]{:S(2)}) copy-start(f32[512]{0:T(512)} %param.18) | copy-start | bytes 6148
  0.0 37.5 %copy-start.4 = (s32[4,512]{1,0:T(4,128)S(1)}, s32[4,512]{1,0:T(4,128)}, u32[]{:S(2)}) copy-start(s32[4,512]{1,0:T(4,128)} %slot_ref.1) | copy-start | bytes 24580
  0.0 37.5 %copy-start.5 = (f32[4,512]{1,0:T(4,128)S(1)}, f32[4,512]{1,0:T(4,128)}, u32[]{:S(2)}) copy-start(f32[4,512]{1,0:T(4,128)} %weight_ref.1) | copy-start | bytes 24580
  0.0 37.5 %copy-start.2 = (f32[100,512]{1,0:T(8,128)S(1)}, f32[100,512]{1,0:T(8,128)}, u32[]{:S(2)}) copy-start(f32[100,512]{1,0:T(8,128)} %dep_ref.1) | copy-start | bytes 614404
  0.0 49.9 %copy-start.1 = (bf16[300,512]{1,0:T(8,128)(2,1)S(1)}, bf16[300,512]{1,0:T(8,128)(2,1)}, u32[]{:S(2)}) copy-start(bf16[300,512]{1,0:T(8,128)(2,1)} %w_in_ref.1) | copy-start | bytes 921604
  0.0 49.9 %copy-start = (bf16[512,512]{1,0:T(8,128)(2,1)S(1)}, bf16[512,512]{1,0:T(8,128)(2,1)}, u32[]{:S(2)}) copy-start(bf16[512,512]{1,0:T(8,128)(2,1)} %w_mid_ref.1) | copy-start | bytes 1572868
  3.5 46.4 %all-to-all-start = ((bf16[128,2,602]{2,1,0:T(2,128)(2,1)}), bf16[128,2,602]{2,1,0:T(2,128)(2,1)S(1)}, u32[]{:S(2)}, u32[]{:S(2)}) async-start(bf16[128,2,602]{2,1,0:T(2,128)(2,1)} %get-tuple-element.20), calls=%async_computation | async-start | bytes 655360 | tf_op jit(solution)/shard_map/all_to_all | solution.py:242
  24.2 3.7 %collective-permute-start = (bf16[8,2,602]{2,1,0:T(2,128)(2,1)}, bf16[8,2,602]{2,1,0:T(2,128)(2,1)S(1)}, u32[]{:S(2)}, u32[]{:S(2)}) collective-permute-start(bf16[8,2,602]{2,1,0:T(2,128)(2,1)} %get-tuple-element.22), channel_id=1, source_target_pairs={{0,4},{4,0},{8,12},{12,8},{16,20},{20,16},{24,28},{28,24},{32,36},... | collective-permute-start | bytes 57800 | tf_op jit(solution)/shard_map/ppermute | solution.py:193
  28.7 11.0 %collective-permute-start.1 = (bf16[8,2,602]{2,1,0:T(2,128)(2,1)S(1)}, bf16[8,2,602]{2,1,0:T(2,128)(2,1)S(1)}, u32[]{:S(2)}, u32[]{:S(2)}) collective-permute-start(bf16[8,2,602]{2,1,0:T(2,128)(2,1)S(1)} %get-tuple-element.44), channel_id=1, source_target_pairs={{0,504},{4,508},{8,0},{12,4},{16,8},{20,12},{24,16},{28,20},{32,24... | collective-permute-start | bytes 57800 | tf_op jit(solution)/shard_map/ppermute | solution.py:197
  35.5 8.4 %collective-permute-start.2 = (bf16[8,2,602]{2,1,0:T(2,128)(2,1)S(1)}, bf16[8,2,602]{2,1,0:T(2,128)(2,1)S(1)}, u32[]{:S(2)}, u32[]{:S(2)}) collective-permute-start(bf16[8,2,602]{2,1,0:T(2,128)(2,1)S(1)} %get-tuple-element.43), channel_id=1, source_target_pairs={{0,8},{4,12},{8,16},{12,20},{16,24},{20,28},{24,32},{28,36},{32,40... | collective-permute-start | bytes 57800 | tf_op jit(solution)/shard_map/ppermute | solution.py:197
  53.5 31.9 %all-to-all-start.1 = ((bf16[128,2,602]{2,1,0:T(2,128)(2,1)}), bf16[128,2,602]{2,1,0:T(2,128)(2,1)S(1)}, u32[]{:S(2)}, u32[]{:S(2)}) async-start(bf16[128,2,602]{2,1,0:T(2,128)(2,1)} %get-tuple-element.30), calls=%async_computation.1 | async-start | bytes 655360 | tf_op jit(solution)/shard_map/all_to_all | solution.py:261
  59.7 3.7 %collective-permute-start.3 = (bf16[8,2,602]{2,1,0:T(2,128)(2,1)}, bf16[8,2,602]{2,1,0:T(2,128)(2,1)S(1)}, u32[]{:S(2)}, u32[]{:S(2)}) collective-permute-start(bf16[8,2,602]{2,1,0:T(2,128)(2,1)} %get-tuple-element.32), channel_id=1, source_target_pairs={{0,4},{4,0},{8,12},{12,8},{16,20},{20,16},{24,28},{28,24},{32,36},... | collective-permute-start | bytes 57800 | tf_op jit(solution)/shard_map/ppermute | solution.py:193
  64.2 8.8 %collective-permute-start.4 = (bf16[8,2,602]{2,1,0:T(2,128)(2,1)S(1)}, bf16[8,2,602]{2,1,0:T(2,128)(2,1)S(1)}, u32[]{:S(2)}, u32[]{:S(2)}) collective-permute-start(bf16[8,2,602]{2,1,0:T(2,128)(2,1)S(1)} %get-tuple-element.41), channel_id=1, source_target_pairs={{0,504},{4,508},{8,0},{12,4},{16,8},{20,12},{24,16},{28,20},{32,24... | collective-permute-start | bytes 57800 | tf_op jit(solution)/shard_map/ppermute | solution.py:197
  71.0 8.4 %collective-permute-start.5 = (bf16[8,2,602]{2,1,0:T(2,128)(2,1)S(1)}, bf16[8,2,602]{2,1,0:T(2,128)(2,1)S(1)}, u32[]{:S(2)}, u32[]{:S(2)}) collective-permute-start(bf16[8,2,602]{2,1,0:T(2,128)(2,1)S(1)} %get-tuple-element.42), channel_id=1, source_target_pairs={{0,8},{4,12},{8,16},{12,20},{16,24},{20,28},{24,32},{28,36},{32,40... | collective-permute-start | bytes 57800 | tf_op jit(solution)/shard_map/ppermute | solution.py:197
